TPU v7x, 768 devices: a whole 4x8x12 slice. The times are simulated.
768 devices in a mesh: energy: 16 (over y, core), kpt: 48 (over z, x).
Axes of the slice: x: 4, y: 8, z: 12, core: 2. Of those that a mesh axis runs over, the one named last changes fastest.
Arguments:
- onsite: float32 [48, 8, 64], P('kpt'), may hold values from -1 to 0
- hamil: float32 [48, 6, 2, 64, 64], P('kpt'), may hold values from -0.5 to 0.5
- coupling: float32 [48, 5, 2, 64, 64], P('kpt'), may hold values from -0.75 to 0.75
- lead_onsite: float32 [32, 48, 2, 2, 64, 64], P('energy', 'kpt'), may hold values from -0.1875 to 0.1875
- lead_hop: float32 [32, 48, 2, 2, 64, 64], P('energy', 'kpt'), may hold values from -0.5 to 2
- counts: int32 [32], replicated, may hold values from 1 to 4
- kernel: float32 [4, 48], replicated, may hold values from -2 to 2
- offsets: int32 [4], replicated, may hold values from 1 to 4
Outputs:
- sigma: float32 [32, 48, 6, 2, 64, 64], P('energy', 'kpt')
- lead_sigma: float32 [32, 48, 2, 2, 64, 64], P('energy', 'kpt')
All inputs are finite; a program needn't handle non-finite values.
Results may differ from a plain program's by a relative error of at most 0.0003.
Values sent between devices are 32-bit elements; how exact they have to be, the bound alone decides.
A program may use at most 128 MiB of HBM per device.

v0:
```python
import jax
import jax.numpy as jnp
from jax import lax
from jax.sharding import PartitionSpec as P

NB = 6
NEWTON = 3
NMODE = 4


BASE_ENERGY = 3.0
BROADENING = 0.1
HIGHEST = lax.Precision.HIGHEST


def cut_along(array, dim, count):
    before, after = (array.shape[:dim], array.shape[dim + 1 :])
    return jnp.moveaxis(array.reshape(*before, count, -1, *after), dim, 0)


def laid_out(blocks, dim):
    blocks = jnp.moveaxis(blocks, 0, dim)
    lengths = blocks.shape
    return blocks.reshape(*lengths[:dim], lengths[dim] * lengths[dim + 1], *lengths[dim + 2 :])


def joined_exchange(array, axis, axes, splits, concats):
    sizes = [lax.axis_size(a) for a in axes]
    blocks = cut_along(array, splits[0], sizes[0])
    blocks = jnp.moveaxis(cut_along(blocks, splits[1] + 1, sizes[1]), 0, 1)
    inside = blocks.shape[2:]
    blocks = blocks.reshape(-1, *inside)
    blocks = lax.all_to_all(blocks, axis, split_axis=0, concat_axis=0, tiled=True)
    blocks = laid_out(blocks.reshape(*sizes, *inside), concats[0] + 1)
    return laid_out(blocks, concats[1])


def product(left_side, right_side):
    return jnp.dot(left_side, right_side, precision=HIGHEST, preferred_element_type=jnp.float32)


def paired(block):
    upper_half = jnp.concatenate([block[0], -block[1]], axis=1)
    lower_half = jnp.concatenate([block[1], block[0]], axis=1)
    return jnp.concatenate([upper_half, lower_half], axis=0)


def compact(matrix):
    width = matrix.shape[0] // 2
    return jnp.stack([matrix[:width, :width], matrix[width:, :width]])


def diagonal_pair(real_part, imag_part):
    return paired(jnp.stack([jnp.diag(real_part), jnp.diag(imag_part)]))


def start_inverse(real_part, imag_part):
    modulus = real_part * real_part + imag_part * imag_part
    return diagonal_pair(real_part / modulus, -imag_part / modulus)


def newton_inverse(matrix, approx):
    doubled = 2.0 * jnp.eye(matrix.shape[0], dtype=jnp.float32)
    for number in range(NEWTON):
        approx = product(approx, doubled - product(matrix, approx))
    return approx


def lead_solve(real_part, imag_part, onsite_block, hop_block, repeats):
    start_guess = start_inverse(real_part, imag_part)
    bare_block = diagonal_pair(real_part, imag_part) - paired(onsite_block)
    hopping = paired(hop_block)

    def advance(number, surface):
        return newton_inverse(
            bare_block - product(hopping.T, product(surface, hopping)), start_guess
        )

    surface = lax.fori_loop(0, repeats, advance, start_guess)
    return compact(product(hopping.T, product(surface, hopping)))


def sweep(real_part, imag_part, hamil_k, coupling_k, left_sigma, right_sigma):
    forward = []
    for segment in range(NB):
        matrix = diagonal_pair(real_part[segment], imag_part[segment]) - paired(hamil_k[segment])
        if segment == 0:
            matrix = matrix - paired(left_sigma)
        if segment == NB - 1:
            matrix = matrix - paired(right_sigma)
        if segment > 0:
            link = paired(coupling_k[segment - 1])
            matrix = matrix - product(link.T, product(forward[-1], link))
        forward.append(
            newton_inverse(matrix, start_inverse(real_part[segment], imag_part[segment]))
        )
    greens = [forward[-1]]
    for segment in range(NB - 2, -1, -1):
        link = paired(coupling_k[segment])
        left_part = product(forward[segment], link)
        right_part = product(link.T, forward[segment])
        greens.insert(0, forward[segment] + product(left_part, product(greens[0], right_part)))
    return jnp.stack([compact(matrix) for matrix in greens])


def convolve(flattened, kernel, offsets):
    energy_count = flattened.shape[0]
    momenta = flattened.shape[1]
    momentum_axis = jnp.arange(momenta, dtype=jnp.int32)
    difference = (momentum_axis[:, None] - momentum_axis[None, :]) % momenta
    selector = (difference[None, :, :] == momentum_axis[:, None, None]).astype(jnp.float32)
    circulant = jnp.einsum("mq,qkj->mkj", kernel, selector, precision=HIGHEST)
    padded = jnp.pad(flattened, ((energy_count, energy_count), (0, 0), (0, 0)))
    result = jnp.zeros_like(flattened)
    for mode_number in range(NMODE):
        offset_now = offsets[mode_number]
        raised = lax.dynamic_slice_in_dim(padded, energy_count + offset_now, energy_count, 0)
        lowered = lax.dynamic_slice_in_dim(padded, energy_count - offset_now, energy_count, 0)
        result = result + jnp.einsum(
            "kj,ejf->ekf", circulant[mode_number], raised + lowered, precision=HIGHEST
        )
    return result


def shards(onsite, hamil, coupling, lead_onsite, lead_hop, counts, kernel, offsets):
    per_device = lead_onsite.shape[0]
    energy_count = counts.shape[0]
    position = lax.axis_index("energy")
    first_energy = position * per_device
    local_onsite = onsite[0]

    def lead_job(energy_id, lead_on, lead_hp):
        energy = BASE_ENERGY + energy_id.astype(jnp.float32) / energy_count
        repeats = counts[energy_id]
        real_part = energy - local_onsite[NB:]
        imag_part = BROADENING * jnp.ones_like(real_part)
        left_sigma = lead_solve(real_part[0], imag_part[0], lead_on[0], lead_hp[0], repeats)
        right_sigma = lead_solve(real_part[1], imag_part[1], lead_on[1], lead_hp[1], repeats)
        return jnp.stack([left_sigma, right_sigma])

    local_ids = first_energy + jnp.arange(per_device, dtype=jnp.int32)

    def single(packed):
        return lead_job(packed[0], packed[1], packed[2])

    lead_sigma = lax.map(single, (local_ids, lead_onsite[:, 0], lead_hop[:, 0]))

    def device_point(energy_id, sigmas):
        energy = BASE_ENERGY + energy_id.astype(jnp.float32) / energy_count
        real_part = energy - local_onsite[:NB]
        imag_part = BROADENING * jnp.ones_like(real_part)
        return sweep(real_part, imag_part, hamil[0], coupling[0], sigmas[0], sigmas[1])

    greens = jax.vmap(device_point)(local_ids, lead_sigma)
    flattened = greens.reshape(per_device, 1, -1)
    spread = joined_exchange(flattened, ("kpt", "energy"), ("kpt", "energy"), (2, 2), (1, 0))
    mixed = convolve(spread, kernel, offsets)
    gathered = lax.all_to_all(
        lax.all_to_all(mixed, "energy", split_axis=0, concat_axis=2, tiled=True),
        "kpt",
        split_axis=1,
        concat_axis=2,
        tiled=True,
    )
    sigma = gathered.reshape((per_device, 1) + greens.shape[1:])
    return (sigma, lead_sigma[:, None])


def solution(mesh):
    placed = (
        P("kpt", None, None),
        P("kpt", None, None, None, None),
        P("kpt", None, None, None, None),
        P("energy", "kpt", None, None, None, None),
        P("energy", "kpt", None, None, None, None),
        P(),
        P(),
        P(),
    )
    return jax.shard_map(
        shards,
        mesh=mesh,
        in_specs=placed,
        out_specs=(
            P("energy", "kpt", None, None, None, None),
            P("energy", "kpt", None, None, None, None),
        ),
        check_vma=False,
    )
```

profile of v0, /device:TPU:1, one launch (start us, length us, event | category | flops | bytes accessed | tf_op | source)
XLA Modules:
  0.0 193.9 jit_solution(11125618859426151888)
XLA Ops:
  0.7 0.8 slice_bitcast_fusion.46
  1.6 1.0 slice_bitcast_fusion.24
  2.8 36.9 %while.32 = (s32[]{:T(128)}, f32[2,2,2,64,64]{4,3,2,1,0:T(8,128)S(1)}, f32[2,2,2,64,64]{4,3,2,1,0:T(8,128)S(1)}, s32[2]{0:T(128)S(1)}, f32[8,64]{1,0:T(8,128)}, ...) while((s32[]{:T(128)}, ...), condition=%wide.region_5.6_spmd, body=%wide.region_0.5_spmd.sunk | while | flops 504177280 | bytes 6362677 | solution.py:146
  4.0 0.7 slice_subtract_fusion.2
  7.7 8.9 %while.34 = (s32[]{:T(128)}, f32[128,128]{1,0:T(8,128)S(1)}, s32[]{:T(128)}, f32[128,128]{1,0:T(8,128)S(1)}, f32[128,128]{0,1:T(8,128)S(1)}, /*index=5*/f32[128,128]{1,0:T(8,128)S(1)}, s32[]{:T(128)}) while((s32[]{:T(128)}, f32[128,128]{1,0:T(8,128)S(1)}, s32[]{:T(128)}, f32[128,128]{1,0:T(8,128)S(1)}, f32[128,128]{0,1:T(8,128)S(1)}, ...), condition=%wide.region_2.2_spmd, body=%wide.region_1.1_spmd.sunk | while | flops 201490432 | bytes 1638477 | solution.py:79
  17.3 8.9 %while.33 = (s32[]{:T(128)}, f32[128,128]{1,0:T(8,128)S(1)}, s32[]{:T(128)}, f32[128,128]{1,0:T(8,128)S(1)}, f32[128,128]{0,1:T(8,128)S(1)}, /*index=5*/f32[128,128]{1,0:T(8,128)S(1)}, s32[]{:T(128)}) while((s32[]{:T(128)}, f32[128,128]{1,0:T(8,128)S(1)}, s32[]{:T(128)}, f32[128,128]{1,0:T(8,128)S(1)}, f32[128,128]{0,1:T(8,128)S(1)}, ...), condition=%wide.region_4.4_spmd, body=%wide.region_3.3_spmd.sunk | while | flops 201490432 | bytes 1638477 | solution.py:79
  27.9 0.7 slice_subtract_fusion.2
  31.6 3.3 %while.34 = (s32[]{:T(128)}, f32[128,128]{1,0:T(8,128)S(1)}, s32[]{:T(128)}, f32[128,128]{1,0:T(8,128)S(1)}, f32[128,128]{0,1:T(8,128)S(1)}, /*index=5*/f32[128,128]{1,0:T(8,128)S(1)}, s32[]{:T(128)}) while((s32[]{:T(128)}, f32[128,128]{1,0:T(8,128)S(1)}, s32[]{:T(128)}, f32[128,128]{1,0:T(8,128)S(1)}, f32[128,128]{0,1:T(8,128)S(1)}, ...), condition=%wide.region_2.2_spmd, body=%wide.region_1.1_spmd.sunk | while | flops 201490432 | bytes 1638477 | solution.py:79
  35.6 3.3 %while.33 = (s32[]{:T(128)}, f32[128,128]{1,0:T(8,128)S(1)}, s32[]{:T(128)}, f32[128,128]{1,0:T(8,128)S(1)}, f32[128,128]{0,1:T(8,128)S(1)}, /*index=5*/f32[128,128]{1,0:T(8,128)S(1)}, s32[]{:T(128)}) while((s32[]{:T(128)}, f32[128,128]{1,0:T(8,128)S(1)}, s32[]{:T(128)}, f32[128,128]{1,0:T(8,128)S(1)}, f32[128,128]{0,1:T(8,128)S(1)}, ...), condition=%wide.region_4.4_spmd, body=%wide.region_3.3_spmd.sunk | while | flops 201490432 | bytes 1638477 | solution.py:79
  39.9 0.9 copy-done.3
  61.9 0.6 copy.99
  62.5 1.6 reshape.337
  64.1 48.5 %all-to-all-start = ((f32[768,1,128]{2,1,0:T(1,128)}), f32[768,1,128]{2,1,0:T(1,128)S(1)}, u32[]{:S(2)}, u32[]{:S(2)}) async-start(f32[768,1,128]{2,1,0:T(1,128)} %reshape.337), calls=%async_computation | async-start | bytes 786432 | tf_op jit(solution)/shard_map/all_to_all | solution.py:33
  112.6 0.6 fusion.140
  123.8 12.9 %all-to-all-done = f32[768,1,128]{2,1,0:T(1,128)S(1)} async-done(((f32[768,1,128]{2,1,0:T(1,128)}), f32[768,1,128]{2,1,0:T(1,128)S(1)}, u32[]{:S(2)}, u32[]{:S(2)}) %all-to-all-start) | async-done | bytes 393248 | tf_op jit(solution)/shard_map/all_to_all | solution.py:33
  137.2 1.6 reduce
  139.5 1.0 fusion.30
  140.6 1.0 convolution_add_fusion.2
  141.6 1.0 convolution_add_fusion.1
  142.7 1.1 fusion.21
  144.2 18.6 %all_to_all.32 = f32[16,1,6144]{2,1,0:T(1,128)S(1)} all-to-all(f32[16,1,6144]{2,1,0:T(1,128)S(1)} %reshape.339), channel_id=1, replica_groups=mesh['energy'=16,'kpt'=48] {'energy'}, dimensions={0} | all-to-all | bytes 786432 | tf_op jit(solution)/shard_map/all_to_all | solution.py:159
  162.8 1.6 reduce.1
  165.8 27.0 %all_to_all.33 = f32[2,48,1024]{2,0,1:T(2,128)S(1)} all-to-all(f32[2,48,1024]{2,0,1:T(2,128)S(1)} %copy.103), channel_id=1, replica_groups=mesh['energy'=16,'kpt'=48] {'kpt'}, dimensions={1} | all-to-all | bytes 786432 | tf_op jit(solution)/shard_map/all_to_all | solution.py:158
  192.9 1.1 reshape.314
  (250 shorter events, 47.3 us)
Async XLA Ops:
  0.6 122.6 %copy-start = (f32[4,48]{1,0:T(4,128)S(1)}, f32[4,48]{1,0:T(4,128)}, u32[]{:S(2)}) copy-start(f32[4,48]{1,0:T(4,128)} %param.20) | copy-start | bytes 2308
  0.6 1.9 %copy-start.2 = (f32[1,6,2,64,64]{4,3,2,1,0:T(8,128)S(1)}, f32[1,6,2,64,64]{4,3,2,1,0:T(8,128)}, u32[]{:S(2)}) copy-start(f32[1,6,2,64,64]{4,3,2,1,0:T(8,128)} %param.15) | copy-start | bytes 589828
  0.7 2.0 %copy-start.4 = (f32[2,1,2,2,64,64]{5,4,3,2,1,0:T(8,128)S(1)}, f32[2,1,2,2,64,64]{5,4,3,2,1,0:T(8,128)}, u32[]{:S(2)}) copy-start(f32[2,1,2,2,64,64]{5,4,3,2,1,0:T(8,128)} %param.17) | copy-start | bytes 393220
  1.6 1.2 copy-start.1
  1.6 1.2 copy-start.7
  39.7 1.1 copy-start.5
  39.8 1.1 copy-start.3
  62.5 50.1 %copy-start.6 = (s32[4]{0:T(128)S(1)}, s32[4]{0:T(128)}, u32[]{:S(2)}) copy-start(s32[4]{0:T(128)} %param.21) | copy-start | bytes 52
  64.1 72.6 %all-to-all-start = ((f32[768,1,128]{2,1,0:T(1,128)}), f32[768,1,128]{2,1,0:T(1,128)S(1)}, u32[]{:S(2)}, u32[]{:S(2)}) async-start(f32[768,1,128]{2,1,0:T(1,128)} %reshape.337), calls=%async_computation | async-start | bytes 786432 | tf_op jit(solution)/shard_map/all_to_all | solution.py:33
where the time goes:
time: 195 us; the launch traced here: 194 us
  starting transfers between devices  48.5 us (25%)
  blocking collectives  45.5 us (23%)
  matrix products  42.2 us (22%)
  local copies, waits for them, and re-layouts  13.7 us (7%)
  waiting for transfers between devices  12.9 us (7%)
  loops' own time  12.8 us (7%)
  between operations  11.6 us (6%)
  other arithmetic  6.71 us (3%)
    all_to_all x1, starting transfers between devices, joined_exchange(): lax.all_to_all(blocks, axis, split_axis=0, concat_axis=0, tiled=True)  48.5 us
    dot_general x133, matrix products, product(): jnp.dot(left_side, right_side, precision=HIGHEST, preferred_element_type=...  37.6 us
    all_to_all x1, blocking collectives, shards(): lax.all_to_all(lax.all_to_all(mixed, 'energy', split_axis=0, concat_axis=...  27 us
    all_to_all x1, blocking collectives, shards(): lax.all_to_all(mixed, 'energy', split_axis=0, concat_axis=2, tiled=True)  18.6 us
    all_to_all x1, waiting for transfers between devices, joined_exchange(): lax.all_to_all(blocks, axis, split_axis=0, concat_axis=0, tiled=True)  12.9 us
    another operation x4, loops' own time, lead_solve(): surface = lax.fori_loop(0, repeats, advance, start_guess)  7.53 us
    another operation x1, loops' own time, shards(): lead_sigma = lax.map(single, (local_ids, lead_onsite[:, 0], lead_hop[:, 0]))  5.26 us
    dot_general x4, matrix products, convolve(): jnp.einsum('kj,ejf->ekf', circulant[mode_number], raised + lowered, preci...  4.16 us
  transfers between devices with their start and end apart: 1, of which 1 were waited for; matrix products, arithmetic and copies ran while one was open for 1% of the time, Pallas kernels for 0%

commit v1 on v0

v1 whole, which is shorter than its diff:
```python
import jax
import jax.numpy as jnp
from jax import lax
from jax.experimental import pallas as pl
from jax.experimental.pallas import tpu as pltpu
from jax.sharding import PartitionSpec as P

NORB = 64
W2 = 128
NB = 6
NMODE = 4
BASE_ENERGY = 3.0
BROADENING = 0.1
F32 = jnp.float32
BF16 = jnp.bfloat16
HIGHEST = lax.Precision.HIGHEST


def paired(real, imag):
    upper = jnp.concatenate([real, -imag], axis=1)
    lower = jnp.concatenate([imag, real], axis=1)
    return jnp.concatenate([upper, lower], axis=0)


def split(x):
    high = x.astype(BF16)
    low = (x - high.astype(F32)).astype(BF16)
    return jnp.concatenate([high, low], axis=1)


def tall(x):
    s = split(x)
    return jnp.concatenate([s, s], axis=0)


def mm(left, right):
    o = jnp.dot(left, right, preferred_element_type=F32)
    return o[:, :W2] + o[:, W2:]


def double(s):
    return jnp.concatenate([s, s], axis=0)


def swap_rows(x):
    return jnp.concatenate([x[NORB:], x[:NORB]], axis=0)


def times_diag(x, arow, brow):
    return x * arow + pltpu.roll(x, NORB, 1) * brow


def diag_times(x, acol, bcol):
    return x * acol + swap_rows(x) * bcol


def compute_kernel(counts_ref, onsite_ref, hamil_ref, coupling_ref, lon_ref, lhop_ref, green_ref, lead_ref,
                   l0_s, tf_s, ts_s, z0_s, sig_s):
    pos = lax.axis_index("energy")
    ids = [pos * 2, pos * 2 + 1]
    reps = [counts_ref[i] for i in ids]
    onsite = onsite_ref[...]
    onsite2 = jnp.concatenate([onsite, onsite], axis=1)
    lane = lax.broadcasted_iota(jnp.int32, (8, W2), 1)
    sign = jnp.where(lane < NORB, 1.0, -1.0).astype(F32)
    arow, brow, acol, bcol = [], [], [], []
    for e in range(2):
        energy = BASE_ENERGY + ids[e].astype(F32) * (1.0 / 32.0)
        re = energy - onsite2
        mod = re * re + BROADENING * BROADENING
        a = re / mod
        b = (-BROADENING / mod) * sign
        arow.append(a)
        brow.append(b)
        acol.append(a.T)
        bcol.append((-b).T)

    chains = [(e, l) for e in range(2) for l in range(2)]
    for c, (e, l) in enumerate(chains):
        hop = paired(lhop_ref[e, l, 0], lhop_ref[e, l, 1])
        l0 = times_diag(hop.T, arow[e][NB + l:NB + l + 1], brow[e][NB + l:NB + l + 1])
        l0_s[c] = l0
        tf_s[c] = hop
        ts_s[c] = split(hop)
        z0_s[c] = paired(lon_ref[e, l, 0], lon_ref[e, l, 1])
        sig_s[c] = mm(split(l0), double(split(hop)))

    def lead_step(number, _):
        r0, l0, sp = [], [], []
        for c, (e, l) in enumerate(chains):
            z = z0_s[c] + sig_s[c]
            r0.append(split(times_diag(z, arow[e][NB + l:NB + l + 1], brow[e][NB + l:NB + l + 1])))
            l0.append(l0_s[c])
        r1, l1 = [], []
        for c in range(4):
            o = mm(jnp.concatenate([r0[c], split(l0[c])], axis=0), double(r0[c]))
            r1.append(split(o[:W2]))
            l1.append(l0[c] + o[W2:])
        r2, l2 = [], []
        for c in range(4):
            o = mm(jnp.concatenate([r1[c], split(l1[c])], axis=0), double(r1[c]))
            r2.append(split(o[:W2]))
            l2.append(split(l1[c] + o[W2:]))
        w = []
        for c in range(4):
            w.append(split(tf_s[c] + mm(r2[c], double(ts_s[c]))))
        for c, (e, l) in enumerate(chains):
            fresh = mm(l2[c], double(w[c]))
            sig_s[c] = jnp.where(number < reps[e], fresh, sig_s[c])
        return 0

    lax.fori_loop(0, jnp.maximum(reps[0], reps[1]), lead_step, 0)

    for c, (e, l) in enumerate(chains):
        s = sig_s[c]
        lead_ref[e, l, 0] = s[:NORB, :NORB]
        lead_ref[e, l, 1] = s[NORB:, :NORB]

    eye = (lax.broadcasted_iota(jnp.int32, (W2, W2), 0) == lax.broadcasted_iota(jnp.int32, (W2, W2), 1)).astype(F32)
    low_lane = lax.broadcasted_iota(jnp.int32, (W2, W2), 1) < NORB
    sigma = [sig_s[0], sig_s[2]]
    gs, lefts, rights = [], [], []
    for b in range(NB - 1):
        link = paired(coupling_ref[b, 0], coupling_ref[b, 1])
        link_t = link.T
        link_s = double(split(link))
        h = paired(hamil_ref[b, 0], hamil_ref[b, 1])
        r0f, r0, l0 = [], [], []
        for e in range(2):
            ar, br = arow[e][b:b + 1], brow[e][b:b + 1]
            r = times_diag(h + sigma[e], ar, br)
            r0f.append(r)
            r0.append(split(r))
            l0.append(times_diag(link_t, ar, br))
        r1f, r1, l1 = [], [], []
        for e in range(2):
            o = mm(jnp.concatenate([r0[e], split(l0[e])], axis=0), double(r0[e]))
            r1f.append(o[:W2])
            r1.append(split(o[:W2]))
            l1.append(l0[e] + o[W2:])
        r2, l2f, l2, q1f, q1 = [], [], [], [], []
        for e in range(2):
            o = mm(jnp.concatenate([r1[e], split(l1[e]), r0[e]], axis=0), double(r1[e]))
            r2.append(split(o[:W2]))
            l2f.append(l1[e] + o[W2:2 * W2])
            l2.append(split(l2f[e]))
            q1f.append(eye + r0f[e] + r1f[e] + o[2 * W2:])
            q1.append(split(q1f[e]))
        o = mm(jnp.concatenate(r2, axis=0), link_s)
        w = [split(link + o[:W2]), split(link + o[W2:])]
        g_b, left_b, right_b = [], [], []
        for e in range(2):
            o = mm(jnp.concatenate([l2[e], q1[e]], axis=0), double(w[e]))
            sigma[e] = o[:W2]
            ac, bc = acol[e][:, b:b + 1], bcol[e][:, b:b + 1]
            left_b.append(split(diag_times(o[W2:], ac, bc)))
        for e in range(2):
            o = mm(jnp.concatenate([l2[e], q1[e]], axis=0), double(r2[e]))
            ac, bc = acol[e][:, b:b + 1], bcol[e][:, b:b + 1]
            right_b.append(double(split(l2f[e] + o[:W2])))
            g_b.append(diag_times(q1f[e] + o[W2:], ac, bc))
        gs.append(g_b)
        lefts.append(left_b)
        rights.append(right_b)

    b = NB - 1
    h = paired(hamil_ref[b, 0], hamil_ref[b, 1])
    green = []
    for e in range(2):
        r0f = times_diag(h + sigma[e] + sig_s[2 * e + 1], arow[e][b:b + 1], brow[e][b:b + 1])
        r0 = split(r0f)
        r1f = mm(r0, double(r0))
        r1 = split(r1f)
        o = mm(jnp.concatenate([r1, r0], axis=0), double(r1))
        q1 = eye + r0f + r1f + o[W2:]
        qf = q1 + mm(split(q1), double(split(o[:W2])))
        green.append(diag_times(qf, acol[e][:, b:b + 1], bcol[e][:, b:b + 1]))

    def put(b, green):
        other = jnp.concatenate([green[1][NORB:], -green[1][:NORB]], axis=0)
        green_ref[b] = jnp.where(low_lane, green[0], other)

    put(b, green)
    for b in range(NB - 2, -1, -1):
        y = [mm(split(green[e]), rights[b][e]) for e in range(2)]
        green = [gs[b][e] + mm(lefts[b][e], double(split(y[e]))) for e in range(2)]
        put(b, green)


def compute(onsite, hamil, coupling, lead_onsite, lead_hop, counts):
    vmem = pl.BlockSpec(memory_space=pltpu.VMEM)
    return pl.pallas_call(
        compute_kernel,
        name="greens",
        out_shape=(
            jax.ShapeDtypeStruct((NB, W2, W2), F32),
            jax.ShapeDtypeStruct((2, 2, 2, NORB, NORB), F32),
        ),
        in_specs=[pl.BlockSpec(memory_space=pltpu.SMEM)] + [vmem] * 5,
        out_specs=(vmem, vmem),
        scratch_shapes=[
            pltpu.VMEM((4, W2, W2), F32),
            pltpu.VMEM((4, W2, W2), F32),
            pltpu.VMEM((4, W2, 2 * W2), BF16),
            pltpu.VMEM((4, W2, W2), F32),
            pltpu.VMEM((4, W2, W2), F32),
        ],
        compiler_params=pltpu.CompilerParams(vmem_limit_bytes=48 * 1024 * 1024),
    )(counts, onsite[0], hamil[0], coupling[0], lead_onsite[:, 0], lead_hop[:, 0])


def cut_along(array, dim, count):
    before, after = (array.shape[:dim], array.shape[dim + 1 :])
    return jnp.moveaxis(array.reshape(*before, count, -1, *after), dim, 0)


def laid_out(blocks, dim):
    blocks = jnp.moveaxis(blocks, 0, dim)
    lengths = blocks.shape
    return blocks.reshape(*lengths[:dim], lengths[dim] * lengths[dim + 1], *lengths[dim + 2 :])


def joined_exchange(array, axis, axes, splits, concats):
    sizes = [lax.axis_size(a) for a in axes]
    blocks = cut_along(array, splits[0], sizes[0])
    blocks = jnp.moveaxis(cut_along(blocks, splits[1] + 1, sizes[1]), 0, 1)
    inside = blocks.shape[2:]
    blocks = blocks.reshape(-1, *inside)
    blocks = lax.all_to_all(blocks, axis, split_axis=0, concat_axis=0, tiled=True)
    blocks = laid_out(blocks.reshape(*sizes, *inside), concats[0] + 1)
    return laid_out(blocks, concats[1])


def convolve(flattened, kernel, offsets):
    energy_count = flattened.shape[0]
    momenta = flattened.shape[1]
    momentum_axis = jnp.arange(momenta, dtype=jnp.int32)
    difference = (momentum_axis[:, None] - momentum_axis[None, :]) % momenta
    selector = (difference[None, :, :] == momentum_axis[:, None, None]).astype(jnp.float32)
    circulant = jnp.einsum("mq,qkj->mkj", kernel, selector, precision=HIGHEST)
    padded = jnp.pad(flattened, ((energy_count, energy_count), (0, 0), (0, 0)))
    result = jnp.zeros_like(flattened)
    for mode_number in range(NMODE):
        offset_now = offsets[mode_number]
        raised = lax.dynamic_slice_in_dim(padded, energy_count + offset_now, energy_count, 0)
        lowered = lax.dynamic_slice_in_dim(padded, energy_count - offset_now, energy_count, 0)
        result = result + jnp.einsum(
            "kj,ejf->ekf", circulant[mode_number], raised + lowered, precision=HIGHEST
        )
    return result


def shards(onsite, hamil, coupling, lead_onsite, lead_hop, counts, kernel, offsets):
    green, lead_sigma = compute(onsite, hamil, coupling, lead_onsite, lead_hop, counts)
    greens = green.reshape(NB, 2, NORB, 2, NORB).transpose(3, 0, 1, 2, 4)
    per_device = greens.shape[0]
    flattened = greens.reshape(per_device, 1, -1)
    spread = joined_exchange(flattened, ("kpt", "energy"), ("kpt", "energy"), (2, 2), (1, 0))
    mixed = convolve(spread, kernel, offsets)
    gathered = lax.all_to_all(
        lax.all_to_all(mixed, "energy", split_axis=0, concat_axis=2, tiled=True),
        "kpt",
        split_axis=1,
        concat_axis=2,
        tiled=True,
    )
    sigma = gathered.reshape((per_device, 1) + greens.shape[1:])
    return (sigma, lead_sigma[:, None])


def solution(mesh):
    placed = (
        P("kpt", None, None),
        P("kpt", None, None, None, None),
        P("kpt", None, None, None, None),
        P("energy", "kpt", None, None, None, None),
        P("energy", "kpt", None, None, None, None),
        P(),
        P(),
        P(),
    )
    return jax.shard_map(
        shards,
        mesh=mesh,
        in_specs=placed,
        out_specs=(
            P("energy", "kpt", None, None, None, None),
            P("energy", "kpt", None, None, None, None),
        ),
        check_vma=False,
    )
```

time: 195 us -> 132 us (0.68)
  matrix products: 42.2 us -> 4.62 us
  starting transfers between devices: 48.5 us -> 31.7 us
  loops' own time: 12.8 us -> 0 us
  Pallas kernels: 0 us -> 9.04 us
  other arithmetic: 6.71 us -> 3.19 us
    dot_general x133 -> x0, matrix products: 37.6 us -> none  [product(): jnp.dot(left_side, right_side, precision=HIGHEST, preferred_element_type=...]
    all_to_all x1, starting transfers between devices: 48.5 us -> 31.7 us  [joined_exchange(): lax.all_to_all(blocks, axis, split_axis=0, concat_axis=0, tiled=True)]
    another operation x5 -> x0, loops' own time: 12.8 us -> none  [the longest x4 7.53 us: lead_solve(): surface = lax.fori_loop(0, repeats, advance, start_guess)]
    pallas_call x0 -> x1, Pallas kernels: none -> 9.04 us  [compute(): pl.pallas_call(compute_kernel, name='greens', out_shape=(jax.ShapeDtypeSt...]
    unnamed x21 -> x20, local copies, waits for them, and re-layouts: 3.96 us -> 8.07 us
    dynamic_slice x4 -> x0, local copies, waits for them, and re-layouts: 2.37 us -> none  [the longest x2 1.19 us: shards(): lead_sigma = lax.map(single, (local_ids, lead_onsite[:, 0], lead_hop[:, 0]))]
where the time goes in v1:
time: 132 us; the launch traced here: 131 us
  blocking collectives  45.5 us (34%)
  starting transfers between devices  31.7 us (24%)
  local copies, waits for them, and re-layouts  13.5 us (10%)
  waiting for transfers between devices  13 us (10%)
  between operations  10.6 us (8%)
  Pallas kernels  9.04 us (7%)
  matrix products  4.62 us (4%)
  other arithmetic  3.19 us (2%)
    all_to_all x1, starting transfers between devices, joined_exchange(): lax.all_to_all(blocks, axis, split_axis=0, concat_axis=0, tiled=True)  31.7 us
    all_to_all x1, blocking collectives, shards(): lax.all_to_all(lax.all_to_all(mixed, 'energy', split_axis=0, concat_axis=...  27 us
    all_to_all x1, blocking collectives, shards(): lax.all_to_all(mixed, 'energy', split_axis=0, concat_axis=2, tiled=True)  18.5 us
    all_to_all x1, waiting for transfers between devices, joined_exchange(): lax.all_to_all(blocks, axis, split_axis=0, concat_axis=0, tiled=True)  13 us
    pallas_call x1, Pallas kernels, compute(): pl.pallas_call(compute_kernel, name='greens', out_shape=(jax.ShapeDtypeSt...  9.04 us
    unnamed x20, local copies, waits for them, and re-layouts  8.07 us
    dot_general x4, matrix products, convolve(): jnp.einsum('kj,ejf->ekf', circulant[mode_number], raised + lowered, preci...  4.16 us
  transfers between devices with their start and end apart: 1, of which 1 were waited for; matrix products, arithmetic and copies ran while one was open for 1% of the time, Pallas kernels for 0%

profile of v1, /device:TPU:1, one launch (start us, length us, event | category | flops | bytes accessed | tf_op | source)
XLA Modules:
  0.0 131.1 jit_solution(6265390160834620785)
XLA Ops:
  0.7 1.0 copy-done.1
  1.7 1.0 copy-done.2
  2.6 0.9 copy-done.3
  3.6 0.9 copy-done.4
  4.5 0.7 copy-done.5
  5.2 0.7 copy-done.6
  5.9 9.0 %greens.1 = (f32[6,128,128]{2,1,0:T(8,128)S(1)}, f32[2,2,2,64,64]{4,3,2,1,0:T(8,128)}) custom-call(s32[32]{0:T(128)S(1)} %copy-done.6, f32[8,64]{1,0:T(8,128)S(1)} %bitcast.72, f32[6,2,64,64]{3,2,1,0:T(8,128)S(1)} %bitcast.68, f32[5,2,64,64]{3,2,1,0:T(8,128)S(1)} %bitcast.69, f32[2,2,2,64,64]{4,3,2,1,0:T(8,128)S(1)} %bitcast.70, ...), custom_call_target="tpu_custom_call" | custom-call | tf_op jit(solution)/shard_map/greens/pallas_call | solution.py:192
  15.9 0.6 copy.28
  16.6 1.6 %reshape.83 = f32[768,1,128]{2,1,0:T(1,128)} reshape(f32[768,1,2,64]{3,2,1,0:T(2,128)S(1)} %bitcast.79) | data formatting | bytes 786432
  18.1 31.7 %all-to-all-start = ((f32[768,1,128]{2,1,0:T(1,128)}), f32[768,1,128]{2,1,0:T(1,128)S(1)}, u32[]{:S(2)}, u32[]{:S(2)}) async-start(f32[768,1,128]{2,1,0:T(1,128)} %reshape.83), calls=%async_computation | async-start | bytes 786432 | tf_op jit(solution)/shard_map/all_to_all | solution.py:229
  49.8 0.7 fusion.26
  60.8 13.0 %all-to-all-done = f32[768,1,128]{2,1,0:T(1,128)S(1)} async-done(((f32[768,1,128]{2,1,0:T(1,128)}), f32[768,1,128]{2,1,0:T(1,128)S(1)}, u32[]{:S(2)}, u32[]{:S(2)}) %all-to-all-start) | async-done | bytes 393248 | tf_op jit(solution)/shard_map/all_to_all | solution.py:229
  73.8 0.5 broadcast.25
  74.3 1.6 %reduce = f32[768,128]{1,0:T(8,128)S(1)} reduce(f32[768,1,128]{2,1,0:T(1,128)S(1)} %all-to-all-done, f32[]{:T(128)} %broadcast.25), dimensions={1}, to_apply=%all_to_all.23.reduce_sub_computation | reduce | bytes 786436 | tf_op jit(solution)/shard_map/all_to_all | solution.py:229
  75.9 0.5 reshape.84
  76.7 1.0 fusion.4
  77.7 1.0 convolution_add_fusion.2
  78.8 1.0 convolution_add_fusion.1
  79.8 1.0 fusion
  80.9 0.5 reshape.85
  81.4 18.5 %all_to_all.32 = f32[16,1,6144]{2,1,0:T(1,128)S(1)} all-to-all(f32[16,1,6144]{2,1,0:T(1,128)S(1)} %reshape.85), channel_id=1, replica_groups=mesh['energy'=16,'kpt'=48] {'energy'}, dimensions={0} | all-to-all | bytes 786432 | tf_op jit(solution)/shard_map/all_to_all | solution.py:261
  99.9 1.6 %reduce.1 = f32[16,6144]{1,0:T(8,128)S(1)} reduce(f32[16,1,6144]{2,1,0:T(1,128)S(1)} %all_to_all.32, f32[]{:T(128)} %broadcast.25), dimensions={1}, to_apply=%all_to_all.24.reduce_sub_computation | reduce | bytes 786436 | tf_op jit(solution)/shard_map/all_to_all | solution.py:261
  102.8 27.0 %all_to_all.33 = f32[2,48,1024]{2,0,1:T(2,128)S(1)} all-to-all(f32[2,48,1024]{2,0,1:T(2,128)S(1)} %copy.32), channel_id=1, replica_groups=mesh['energy'=16,'kpt'=48] {'kpt'}, dimensions={1} | all-to-all | bytes 786432 | tf_op jit(solution)/shard_map/all_to_all | solution.py:260
  130.0 1.1 reshape.77
  (24 shorter events, 3.3 us)
Async XLA Ops:
  0.6 59.6 %copy-start = (f32[4,48]{1,0:T(4,128)S(1)}, f32[4,48]{1,0:T(4,128)}, u32[]{:S(2)}) copy-start(f32[4,48]{1,0:T(4,128)} %param.14) | copy-start | bytes 2308
  0.6 1.0 copy-start.1
  1.6 1.0 copy-start.2
  2.6 0.9 copy-start.3
  3.6 0.9 copy-start.4
  4.5 0.7 copy-start.5
  5.2 0.7 copy-start.6
  16.6 33.3 %copy-start.7 = (s32[4]{0:T(128)S(1)}, s32[4]{0:T(128)}, u32[]{:S(2)}) copy-start(s32[4]{0:T(128)} %param.15) | copy-start | bytes 52
  18.1 55.6 %all-to-all-start = ((f32[768,1,128]{2,1,0:T(1,128)}), f32[768,1,128]{2,1,0:T(1,128)S(1)}, u32[]{:S(2)}, u32[]{:S(2)}) async-start(f32[768,1,128]{2,1,0:T(1,128)} %reshape.83), calls=%async_computation | async-start | bytes 786432 | tf_op jit(solution)/shard_map/all_to_all | solution.py:229

commit v2 on v1

--- a/solution.py
+++ b/solution.py
@@ -209,63 +209,181 @@
     )(counts, onsite[0], hamil[0], coupling[0], lead_onsite[:, 0], lead_hop[:, 0])
 
 
-def cut_along(array, dim, count):
-    before, after = (array.shape[:dim], array.shape[dim + 1 :])
-    return jnp.moveaxis(array.reshape(*before, count, -1, *after), dim, 0)
-
-
-def laid_out(blocks, dim):
-    blocks = jnp.moveaxis(blocks, 0, dim)
-    lengths = blocks.shape
-    return blocks.reshape(*lengths[:dim], lengths[dim] * lengths[dim + 1], *lengths[dim + 2 :])
-
-
-def joined_exchange(array, axis, axes, splits, concats):
-    sizes = [lax.axis_size(a) for a in axes]
-    blocks = cut_along(array, splits[0], sizes[0])
-    blocks = jnp.moveaxis(cut_along(blocks, splits[1] + 1, sizes[1]), 0, 1)
-    inside = blocks.shape[2:]
-    blocks = blocks.reshape(-1, *inside)
-    blocks = lax.all_to_all(blocks, axis, split_axis=0, concat_axis=0, tiled=True)
-    blocks = laid_out(blocks.reshape(*sizes, *inside), concats[0] + 1)
-    return laid_out(blocks, concats[1])
-
-
-def convolve(flattened, kernel, offsets):
-    energy_count = flattened.shape[0]
-    momenta = flattened.shape[1]
-    momentum_axis = jnp.arange(momenta, dtype=jnp.int32)
-    difference = (momentum_axis[:, None] - momentum_axis[None, :]) % momenta
-    selector = (difference[None, :, :] == momentum_axis[:, None, None]).astype(jnp.float32)
-    circulant = jnp.einsum("mq,qkj->mkj", kernel, selector, precision=HIGHEST)
-    padded = jnp.pad(flattened, ((energy_count, energy_count), (0, 0), (0, 0)))
-    result = jnp.zeros_like(flattened)
-    for mode_number in range(NMODE):
-        offset_now = offsets[mode_number]
-        raised = lax.dynamic_slice_in_dim(padded, energy_count + offset_now, energy_count, 0)
-        lowered = lax.dynamic_slice_in_dim(padded, energy_count - offset_now, energy_count, 0)
-        result = result + jnp.einsum(
-            "kj,ejf->ekf", circulant[mode_number], raised + lowered, precision=HIGHEST
-        )
-    return result
+MESH = pl.DeviceIdType.MESH
+NK = 48
+NZ = 12
+NX = 4
+NY = 8
+TILES = 2 * NK
+
+
+def ring_step(n):
+    half = lax.div(n + 1, 2)
+    return jnp.where(lax.rem(n, 2) == 1, 6 - half, 6 + half)
+
+
+def position():
+    pos, k = lax.axis_index("energy"), lax.axis_index("kpt")
+    return lax.div(pos, 2), lax.rem(pos, 2), lax.div(k, NX), lax.rem(k, NX)
+
+
+def greet():
+    y, c, z, x = position()
+    barrier = pltpu.get_barrier_semaphore()
+    me = c * NK + z * NX + x
+
+    def one(i, _):
+        t = lax.rem(me + i, TILES)
+        pl.semaphore_signal(barrier, inc=1, device_id=(y * 2 + lax.div(t, NK), lax.rem(t, NK)), device_id_type=MESH)
+        return 0
+
+    lax.fori_loop(1, TILES, one, 0)
+    for step in (1, NY - 1):
+        there = lax.rem(y + step, NY)
+        pl.semaphore_signal(barrier, inc=1, device_id=(there * 2 + c, z * NX + x), device_id_type=MESH)
+
+
+def all_greeted():
+    pl.semaphore_wait(pltpu.get_barrier_semaphore(), TILES + 1)
+
+
+def scatter(src, dst, send_sem, recv_sem, grouped):
+    y, c, z, x = position()
+    me = c * NK + z * NX + x
+
+    def one(i, _):
+        n = lax.div(i, 8)
+        zz = lax.rem(z + ring_step(n), NZ)
+        r = lax.rem(i, 8)
+        xx = lax.rem(x + lax.div(r, 2), NX)
+        cc = lax.rem(c + lax.rem(r, 2), 2)
+        kk = zz * NX + xx
+        pltpu.make_async_remote_copy(
+            src_ref=src.at[cc * NK + kk],
+            dst_ref=dst.at[me],
+            send_sem=send_sem,
+            recv_sem=recv_sem.at[n] if grouped else recv_sem,
+            device_id=(y * 2 + cc, kk),
+            device_id_type=MESH,
+        ).start()
+        return 0
+
+    lax.fori_loop(0, TILES - 8, one, 0)
+    lax.fori_loop(TILES - 7, TILES, one, 0)
+    pltpu.make_async_copy(src.at[me], dst.at[me], recv_sem.at[NZ - 1] if grouped else recv_sem).start()
+
+
+def wait_tiles(ref, count, sem):
+    part = ref.at[pl.ds(0, count)]
+    pltpu.make_async_copy(part, part, sem).wait()
+
+
+def exchange_body(green_ref, mix_ref, sigma_ref, here, below, above, mixed, send_a, recv_a, send_b, recv_b, send_c, recv_c):
+    y, c, z, x = position()
+    scatter(green_ref, here, send_a, recv_a, True)
+
+    def forward(n, _):
+        wait_tiles(here, 8, recv_a.at[n])
+        zs = lax.rem(z - ring_step(n) + NZ, NZ)
+        for core in range(2):
+            rows = pl.ds(core * NK + zs * NX, NX)
+            for step, there, slot in ((1, below, 0), (NY - 1, above, 1)):
+                pltpu.make_async_remote_copy(
+                    src_ref=here.at[rows],
+                    dst_ref=there.at[rows],
+                    send_sem=send_b.at[slot],
+                    recv_sem=recv_b.at[slot],
+                    device_id=(lax.rem(y + step, NY) * 2 + c, z * NX + x),
+                    device_id_type=MESH,
+                ).start()
+        return 0
+
+    lax.fori_loop(0, NZ, forward, 0)
+    wait_tiles(below, TILES, recv_b.at[0])
+    wait_tiles(above, TILES, recv_b.at[1])
+
+    mix = mix_ref[...]
+    mix_high = mix.astype(BF16)
+    mix = jnp.concatenate([mix_high, (mix - mix_high.astype(F32)).astype(BF16)], axis=0)
+    first = lax.broadcasted_iota(jnp.int32, (NK, W2), 1) < NORB
+    low = jnp.where(y > 0, 1.0, 0.0).astype(F32)
+    high = jnp.where(y < NY - 1, 1.0, 0.0).astype(F32)
+    flat = [r.reshape(TILES * 8, W2) for r in (below, here, above)]
+    out = mixed.reshape(TILES * 8, W2)
+    for s in range(8):
+        t = []
+        for r, keep in zip(flat, (low, None, high)):
+            for core in range(2):
+                v = r[pl.ds(core * NK * 8 + s, NK, stride=8), :]
+                t.append(v if keep is None else v * keep)
+        w = [pltpu.roll(v, NORB, 1) for v in t]
+        for core in range(2):
+            q = 2 + core
+            x1 = w[q] + jnp.where(first, w[q - 1], w[q + 1])
+            x2 = t[q + 1] + t[q - 1]
+            x3 = jnp.where(first, w[q + 1] + w[q - 2], w[q + 2] + w[q - 1])
+            x4 = t[q + 2] + t[q - 2]
+            xs = split(jnp.concatenate([x1, x2, x3, x4], axis=0))
+            o = jnp.dot(mix, xs, preferred_element_type=F32)
+            o = o[:, :W2] + o[:, W2:]
+            out[pl.ds(core * NK * 8 + s, NK, stride=8), :] = o[:NK] + o[NK:]
+
+    scatter(mixed, sigma_ref, send_c, recv_c, False)
+    wait_tiles(here, TILES - 1, send_a)
+    wait_tiles(below, TILES, send_b.at[0])
+    wait_tiles(above, TILES, send_b.at[1])
+    wait_tiles(sigma_ref, TILES, recv_c)
+    wait_tiles(mixed, TILES - 1, send_c)
+
+
+def mix_rows(kernel, offsets):
+    steps = jnp.arange(1, NMODE + 1, dtype=jnp.int32)
+    chosen = jnp.where(offsets[None, :] == steps[:, None], 1.0, 0.0).astype(F32)
+    by_step = jnp.sum(chosen[:, :, None] * kernel[None, :, :], axis=1)
+    k = jnp.arange(NK, dtype=jnp.int32)
+    selector = (((k[:, None] - k[None, :]) % NK)[None] == k[:, None, None]).astype(F32)
+    return jnp.einsum("oq,qkj->koj", by_step, selector, precision=HIGHEST).reshape(NK, NMODE * NK)
+
+
+SCRATCH = [
+    pltpu.VMEM((TILES, 8, W2), F32),
+    pltpu.VMEM((TILES, 8, W2), F32),
+    pltpu.VMEM((TILES, 8, W2), F32),
+    pltpu.VMEM((TILES, 8, W2), F32),
+    pltpu.SemaphoreType.DMA,
+    pltpu.SemaphoreType.DMA((NZ,)),
+    pltpu.SemaphoreType.DMA((2,)),
+    pltpu.SemaphoreType.DMA((2,)),
+    pltpu.SemaphoreType.DMA,
+    pltpu.SemaphoreType.DMA,
+]
+
+
+def exchange_kernel(*refs):
+    greet()
+    all_greeted()
+    exchange_body(*refs)
+
+
+def exchange(green, mix):
+    vmem = pl.BlockSpec(memory_space=pltpu.VMEM)
+    return pl.pallas_call(
+        exchange_kernel,
+        name="exchange",
+        out_shape=jax.ShapeDtypeStruct((TILES, 8, W2), F32),
+        in_specs=[vmem] * 2,
+        out_specs=vmem,
+        scratch_shapes=SCRATCH,
+        compiler_params=pltpu.CompilerParams(collective_id=0, has_side_effects=True),
+    )(green, mix)
 
 
 def shards(onsite, hamil, coupling, lead_onsite, lead_hop, counts, kernel, offsets):
+    mix = mix_rows(kernel, offsets)
     green, lead_sigma = compute(onsite, hamil, coupling, lead_onsite, lead_hop, counts)
-    greens = green.reshape(NB, 2, NORB, 2, NORB).transpose(3, 0, 1, 2, 4)
-    per_device = greens.shape[0]
-    flattened = greens.reshape(per_device, 1, -1)
-    spread = joined_exchange(flattened, ("kpt", "energy"), ("kpt", "energy"), (2, 2), (1, 0))
-    mixed = convolve(spread, kernel, offsets)
-    gathered = lax.all_to_all(
-        lax.all_to_all(mixed, "energy", split_axis=0, concat_axis=2, tiled=True),
-        "kpt",
-        split_axis=1,
-        concat_axis=2,
-        tiled=True,
-    )
-    sigma = gathered.reshape((per_device, 1) + greens.shape[1:])
-    return (sigma, lead_sigma[:, None])
+    sigma = exchange(green.reshape(TILES, 8, W2), mix)
+    sigma = sigma.reshape(NB, 2, NORB, 2, NORB).transpose(3, 0, 1, 2, 4)
+    return (sigma[:, None], lead_sigma[:, None])
 
 
 def solution(mesh):

time: 132 us -> 86.1 us (0.65)
  Pallas kernels: 9.04 us -> 73.7 us
  blocking collectives: 45.5 us -> 0 us
  starting transfers between devices: 31.7 us -> 0 us
  waiting for transfers between devices: 13 us -> 0 us
  between operations: 10.6 us -> 0.67 us
  local copies, waits for them, and re-layouts: 13.5 us -> 9.11 us
  matrix products: 4.62 us -> 0.46 us
  other arithmetic: 3.19 us -> 1.52 us
    pallas_call x0 -> x1, Pallas kernels: none -> 63.7 us  [exchange(): pl.pallas_call(exchange_kernel, name='exchange', out_shape=jax.ShapeDtype...]
    all_to_all x2 -> x0, blocking collectives: 45.5 us -> none  [the longest x1 27 us: shards(): lax.all_to_all(lax.all_to_all(mixed, 'energy', split_axis=0, concat_axis=...]
    all_to_all x1 -> x0, starting transfers between devices: 31.7 us -> none  [joined_exchange(): lax.all_to_all(blocks, axis, split_axis=0, concat_axis=0, tiled=True)]
    all_to_all x1 -> x0, waiting for transfers between devices: 13 us -> none  [joined_exchange(): lax.all_to_all(blocks, axis, split_axis=0, concat_axis=0, tiled=True)]
    dot_general x5 -> x1, matrix products: 4.62 us -> 0.46 us  [mix_rows(): jnp.einsum('oq,qkj->koj', by_step, selector, precision=HIGHEST)]
    all_to_all x2 -> x0, other arithmetic: 3.17 us -> none  [the longest x1 1.59 us: shards(): lax.all_to_all(mixed, 'energy', split_axis=0, concat_axis=2, tiled=True)]
    unnamed x20 -> x14, local copies, waits for them, and re-layouts: 8.07 us -> 5.95 us
    all_to_all x6 -> x0, local copies, waits for them, and re-layouts: 1.71 us -> none  [the longest x3 1.01 us: shards(): lax.all_to_all(mixed, 'energy', split_axis=0, concat_axis=2, tiled=True)]
  transfers between devices with their start and end apart: 1 -> 0, of which waited for: 1 -> 0; matrix products, arithmetic and copies ran while one was open for 1% -> 0% of each run, Pallas kernels for 0% -> 0%
where the time goes in v2:
time: 86.1 us; the launch traced here: 85.4 us
  Pallas kernels  73.7 us (86%)
  local copies, waits for them, and re-layouts  9.11 us (11%)
  other arithmetic  1.52 us (2%)
    pallas_call x1, Pallas kernels, exchange(): pl.pallas_call(exchange_kernel, name='exchange', out_shape=jax.ShapeDtype...  63.7 us
    pallas_call x1, Pallas kernels, compute(): pl.pallas_call(compute_kernel, name='greens', out_shape=(jax.ShapeDtypeSt...  9.93 us
    unnamed x14, local copies, waits for them, and re-layouts  5.95 us
    reshape x2, local copies, waits for them, and re-layouts, shards(): sigma = sigma.reshape(NB, 2, NORB, 2, NORB).transpose(3, 0, 1, 2, 4)  2.44 us

profile of v2, /device:TPU:1, one launch (start us, length us, event | category | flops | bytes accessed | tf_op | source)
XLA Modules:
  0.0 85.4 jit_solution(5274748206862655175)
XLA Ops:
  0.6 0.7 compare_select_fusion
  1.4 0.8 multiply_reduce_fusion
  2.2 0.5 fusion.1
  2.6 0.7 reshape.64.refs_1_
  3.3 0.0 copy-start.1
  3.3 1.0 %copy-done.1 = f32[1,6,2,64,64]{4,3,2,1,0:T(8,128)S(1)} copy-done((f32[1,6,2,64,64]{4,3,2,1,0:T(8,128)S(1)}, f32[1,6,2,64,64]{4,3,2,1,0:T(8,128)}, u32[]{:S(2)}) %copy-start.1) | copy-done | bytes 196632
  4.3 0.0 copy-start.2
  4.3 1.0 %copy-done.2 = f32[1,5,2,64,64]{4,3,2,1,0:T(8,128)S(1)} copy-done((f32[1,5,2,64,64]{4,3,2,1,0:T(8,128)S(1)}, f32[1,5,2,64,64]{4,3,2,1,0:T(8,128)}, u32[]{:S(2)}) %copy-start.2) | copy-done | bytes 163864
  5.3 0.0 copy-start.3
  5.3 0.9 %copy-done.3 = f32[2,1,2,2,64,64]{5,4,3,2,1,0:T(8,128)S(1)} copy-done((f32[2,1,2,2,64,64]{5,4,3,2,1,0:T(8,128)S(1)}, f32[2,1,2,2,64,64]{5,4,3,2,1,0:T(8,128)}, u32[]{:S(2)}) %copy-start.3) | copy-done | bytes 131096
  6.3 0.0 copy-start.4
  6.3 0.9 %copy-done.4 = f32[2,1,2,2,64,64]{5,4,3,2,1,0:T(8,128)S(1)} copy-done((f32[2,1,2,2,64,64]{5,4,3,2,1,0:T(8,128)S(1)}, f32[2,1,2,2,64,64]{5,4,3,2,1,0:T(8,128)}, u32[]{:S(2)}) %copy-start.4) | copy-done | bytes 131096
  7.2 0.0 copy-start.5
  7.2 0.7 copy-done.5
  7.9 0.0 copy-start.6
  7.9 0.7 copy-done.6
  8.6 9.9 %greens.1 = (f32[6,128,128]{2,1,0:T(8,128)S(1)}, f32[2,2,2,64,64]{4,3,2,1,0:T(8,128)}) custom-call(s32[32]{0:T(128)S(1)} %copy-done.6, f32[8,64]{1,0:T(8,128)S(1)} %bitcast.24, f32[6,2,64,64]{3,2,1,0:T(8,128)S(1)} %bitcast.20, f32[5,2,64,64]{3,2,1,0:T(8,128)S(1)} %bitcast.21, f32[2,2,2,64,64]{4,3,2,1,0:T(8,128)S(1)} %bitcast.22, ...), custom_call_target="tpu_custom_call" | custom-call | tf_op jit(solution)/shard_map/greens/pallas_call | solution.py:192
  18.5 0.0 copy-start
  18.5 0.7 copy-done
  19.2 63.7 %exchange.1 = f32[96,8,128]{2,1,0:T(8,128)} custom-call(f32[96,8,128]{2,1,0:T(8,128)} %bitcast.19, f32[48,192]{1,0:T(8,128)} %reshape.64.refs_1_), custom_call_target="tpu_custom_call" | custom-call | tf_op jit(solution)/shard_map/exchange/pallas_call | solution.py:370
  83.0 1.5 %reshape.65 = f32[6,2,64,2,64]{4,3,2,1,0:T(2,128)S(1)} reshape(f32[96,8,128]{2,1,0:T(8,128)} %exchange.1) | data formatting | bytes 786432 | tf_op jit(solution)/shard_map/reshape | solution.py:385
  84.4 1.0 %copy.15 = f32[6,2,64,2,64]{4,2,1,0,3:T(8,128)} copy(f32[6,2,64,2,64]{4,3,2,1,0:T(2,128)S(1)} %reshape.65) | data formatting | bytes 786432 | tf_op jit(solution)/shard_map/reshape | solution.py:385
  (2 shorter events, 0.0 us)
Async XLA Ops:
  3.3 1.0 %copy-start.1 = (f32[1,6,2,64,64]{4,3,2,1,0:T(8,128)S(1)}, f32[1,6,2,64,64]{4,3,2,1,0:T(8,128)}, u32[]{:S(2)}) copy-start(f32[1,6,2,64,64]{4,3,2,1,0:T(8,128)} %param.9) | copy-start | bytes 589828
  4.3 1.0 %copy-start.2 = (f32[1,5,2,64,64]{4,3,2,1,0:T(8,128)S(1)}, f32[1,5,2,64,64]{4,3,2,1,0:T(8,128)}, u32[]{:S(2)}) copy-start(f32[1,5,2,64,64]{4,3,2,1,0:T(8,128)} %param.10) | copy-start | bytes 491524
  5.3 0.9 %copy-start.3 = (f32[2,1,2,2,64,64]{5,4,3,2,1,0:T(8,128)S(1)}, f32[2,1,2,2,64,64]{5,4,3,2,1,0:T(8,128)}, u32[]{:S(2)}) copy-start(f32[2,1,2,2,64,64]{5,4,3,2,1,0:T(8,128)} %param.11) | copy-start | bytes 393220
  6.3 0.9 %copy-start.4 = (f32[2,1,2,2,64,64]{5,4,3,2,1,0:T(8,128)S(1)}, f32[2,1,2,2,64,64]{5,4,3,2,1,0:T(8,128)}, u32[]{:S(2)}) copy-start(f32[2,1,2,2,64,64]{5,4,3,2,1,0:T(8,128)} %param.12) | copy-start | bytes 393220
  7.2 0.7 copy-start.5
  7.9 0.7 copy-start.6
  18.5 0.7 copy-start

commit v3 on v2

--- a/solution.py
+++ b/solution.py
@@ -9,6 +9,7 @@
 W2 = 128
 NB = 6
 NMODE = 4
+MAXIT = 4
 BASE_ENERGY = 3.0
 BROADENING = 0.1
 F32 = jnp.float32
@@ -54,9 +55,10 @@
     return x * acol + swap_rows(x) * bcol
 
 
-def compute_kernel(counts_ref, onsite_ref, hamil_ref, coupling_ref, lon_ref, lhop_ref, green_ref, lead_ref,
-                   l0_s, tf_s, ts_s, z0_s, sig_s):
+def compute_body(counts_ref, onsite_ref, hamil_ref, coupling_ref, lon_ref, lhop_ref, green_ref, lead_ref,
+                 l0_s, tf_s, ts_s, z0_s, sig_s, loaded):
     pos = lax.axis_index("energy")
+    loaded(0)
     ids = [pos * 2, pos * 2 + 1]
     reps = [counts_ref[i] for i in ids]
     onsite = onsite_ref[...]
@@ -75,6 +77,7 @@
         acol.append(a.T)
         bcol.append((-b).T)
 
+    loaded(1)
     chains = [(e, l) for e in range(2) for l in range(2)]
     for c, (e, l) in enumerate(chains):
         hop = paired(lhop_ref[e, l, 0], lhop_ref[e, l, 1])
@@ -109,13 +112,14 @@
             sig_s[c] = jnp.where(number < reps[e], fresh, sig_s[c])
         return 0
 
-    lax.fori_loop(0, jnp.maximum(reps[0], reps[1]), lead_step, 0)
+    lax.fori_loop(0, MAXIT, lead_step, 0)
 
     for c, (e, l) in enumerate(chains):
         s = sig_s[c]
         lead_ref[e, l, 0] = s[:NORB, :NORB]
         lead_ref[e, l, 1] = s[NORB:, :NORB]
 
+    loaded(2)
     eye = (lax.broadcasted_iota(jnp.int32, (W2, W2), 0) == lax.broadcasted_iota(jnp.int32, (W2, W2), 1)).astype(F32)
     low_lane = lax.broadcasted_iota(jnp.int32, (W2, W2), 1) < NORB
     sigma = [sig_s[0], sig_s[2]]
@@ -178,35 +182,13 @@
 
     def put(b, green):
         other = jnp.concatenate([green[1][NORB:], -green[1][:NORB]], axis=0)
-        green_ref[b] = jnp.where(low_lane, green[0], other)
+        green_ref[pl.ds(b * 16, 16)] = jnp.where(low_lane, green[0], other).reshape(16, 8, W2)
 
     put(b, green)
     for b in range(NB - 2, -1, -1):
         y = [mm(split(green[e]), rights[b][e]) for e in range(2)]
         green = [gs[b][e] + mm(lefts[b][e], double(split(y[e]))) for e in range(2)]
         put(b, green)
-
-
-def compute(onsite, hamil, coupling, lead_onsite, lead_hop, counts):
-    vmem = pl.BlockSpec(memory_space=pltpu.VMEM)
-    return pl.pallas_call(
-        compute_kernel,
-        name="greens",
-        out_shape=(
-            jax.ShapeDtypeStruct((NB, W2, W2), F32),
-            jax.ShapeDtypeStruct((2, 2, 2, NORB, NORB), F32),
-        ),
-        in_specs=[pl.BlockSpec(memory_space=pltpu.SMEM)] + [vmem] * 5,
-        out_specs=(vmem, vmem),
-        scratch_shapes=[
-            pltpu.VMEM((4, W2, W2), F32),
-            pltpu.VMEM((4, W2, W2), F32),
-            pltpu.VMEM((4, W2, 2 * W2), BF16),
-            pltpu.VMEM((4, W2, W2), F32),
-            pltpu.VMEM((4, W2, W2), F32),
-        ],
-        compiler_params=pltpu.CompilerParams(vmem_limit_bytes=48 * 1024 * 1024),
-    )(counts, onsite[0], hamil[0], coupling[0], lead_onsite[:, 0], lead_hop[:, 0])
 
 
 MESH = pl.DeviceIdType.MESH
@@ -217,60 +199,74 @@
 TILES = 2 * NK
 
 
+def around(i, n):
+    return jnp.where(i >= n, i - n, i)
+
+
 def ring_step(n):
-    half = lax.div(n + 1, 2)
-    return jnp.where(lax.rem(n, 2) == 1, 6 - half, 6 + half)
-
-
-def position():
-    pos, k = lax.axis_index("energy"), lax.axis_index("kpt")
-    return lax.div(pos, 2), lax.rem(pos, 2), lax.div(k, NX), lax.rem(k, NX)
-
-
-def greet():
-    y, c, z, x = position()
+    half = (n + 1) >> 1
+    return jnp.where((n & 1) == 1, 6 - half, 6 + half)
+
+
+class Place:
+    def __init__(self):
+        pos, k = lax.axis_index("energy"), lax.axis_index("kpt")
+        self.y, self.c, self.z, self.x, self.k = pos >> 1, pos & 1, k >> 2, k & 3, k
+        self.me = self.c * NK + k
+        self.peers = [((self.x + dx) & 3, self.c ^ dc) for dx in range(NX) for dc in range(2)]
+        self.up = (around(self.y + 1, NY) * 2 + self.c, k)
+        self.down = (around(self.y + NY - 1, NY) * 2 + self.c, k)
+
+    def device(self, zz, r):
+        xx, cc = self.peers[r]
+        return self.y * 2 + cc, zz * NX + xx
+
+    def tile(self, zz, r):
+        xx, cc = self.peers[r]
+        return cc * NK + zz * NX + xx
+
+
+def greet(here):
     barrier = pltpu.get_barrier_semaphore()
-    me = c * NK + z * NX + x
-
-    def one(i, _):
-        t = lax.rem(me + i, TILES)
-        pl.semaphore_signal(barrier, inc=1, device_id=(y * 2 + lax.div(t, NK), lax.rem(t, NK)), device_id_type=MESH)
+
+    def layer(n, _):
+        zz = around(here.z + n, NZ)
+        for r in range(8):
+            pl.semaphore_signal(barrier, inc=1, device_id=here.device(zz, r), device_id_type=MESH)
         return 0
 
-    lax.fori_loop(1, TILES, one, 0)
-    for step in (1, NY - 1):
-        there = lax.rem(y + step, NY)
-        pl.semaphore_signal(barrier, inc=1, device_id=(there * 2 + c, z * NX + x), device_id_type=MESH)
+    for r in range(1, 8):
+        pl.semaphore_signal(barrier, inc=1, device_id=here.device(here.z, r), device_id_type=MESH)
+    for there in (here.up, here.down):
+        pl.semaphore_signal(barrier, inc=1, device_id=there, device_id_type=MESH)
+    lax.fori_loop(1, NZ, layer, 0)
 
 
 def all_greeted():
     pl.semaphore_wait(pltpu.get_barrier_semaphore(), TILES + 1)
 
 
-def scatter(src, dst, send_sem, recv_sem, grouped):
-    y, c, z, x = position()
-    me = c * NK + z * NX + x
-
-    def one(i, _):
-        n = lax.div(i, 8)
-        zz = lax.rem(z + ring_step(n), NZ)
-        r = lax.rem(i, 8)
-        xx = lax.rem(x + lax.div(r, 2), NX)
-        cc = lax.rem(c + lax.rem(r, 2), 2)
-        kk = zz * NX + xx
+def scatter(here, src, dst, send_sem, recv_of):
+    def send(n, zz, r):
         pltpu.make_async_remote_copy(
-            src_ref=src.at[cc * NK + kk],
-            dst_ref=dst.at[me],
+            src_ref=src.at[here.tile(zz, r)],
+            dst_ref=dst.at[here.me],
             send_sem=send_sem,
-            recv_sem=recv_sem.at[n] if grouped else recv_sem,
-            device_id=(y * 2 + cc, kk),
+            recv_sem=recv_of(n),
+            device_id=here.device(zz, r),
             device_id_type=MESH,
         ).start()
+
+    def layer(n, _):
+        zz = around(here.z + ring_step(n), NZ)
+        for r in range(8):
+            send(n, zz, r)
         return 0
 
-    lax.fori_loop(0, TILES - 8, one, 0)
-    lax.fori_loop(TILES - 7, TILES, one, 0)
-    pltpu.make_async_copy(src.at[me], dst.at[me], recv_sem.at[NZ - 1] if grouped else recv_sem).start()
+    lax.fori_loop(0, NZ - 1, layer, 0)
+    for r in range(1, 8):
+        send(NZ - 1, here.z, r)
+    pltpu.make_async_copy(src.at[here.me], dst.at[here.me], recv_of(NZ - 1)).start()
 
 
 def wait_tiles(ref, count, sem):
@@ -278,22 +274,49 @@
     pltpu.make_async_copy(part, part, sem).wait()
 
 
-def exchange_body(green_ref, mix_ref, sigma_ref, here, below, above, mixed, send_a, recv_a, send_b, recv_b, send_c, recv_c):
-    y, c, z, x = position()
-    scatter(green_ref, here, send_a, recv_a, True)
+def mix_rows(kernel_ref, offsets_ref):
+    q = lax.broadcasted_iota(jnp.int32, (NK, W2), 0)
+    i = lax.broadcasted_iota(jnp.int32, (NK, W2), 1)
+    total = q + i
+    turn = ((total == 0) | (total == NK) | (total == 2 * NK) | (total == 3 * NK)).astype(BF16)
+    kernel = kernel_ref[...]
+    rows = []
+    for o in range(1, NMODE + 1):
+        row = jnp.zeros((1, NK), F32)
+        for m in range(NMODE):
+            row = row + jnp.where(offsets_ref[m] == o, kernel[m:m + 1], 0.0)
+        rows.append(row)
+    rows = jnp.concatenate(rows + rows, axis=0)
+    high = rows.astype(BF16)
+    low = (rows - high.astype(F32)).astype(BF16)
+    ext = jnp.dot(high, turn, preferred_element_type=F32) + jnp.dot(low, turn, preferred_element_type=F32)
+    parts = []
+    for o in (0, 2):
+        a = jnp.broadcast_to(ext[o:o + 1], (NK, W2))
+        b = jnp.broadcast_to(ext[o + 1:o + 2], (NK, W2))
+        a = pltpu.roll(a, W2 - NK, 1, stride=1, stride_axis=0)
+        b = pltpu.roll(b, 0, 1, stride=1, stride_axis=0)
+        parts.append(jnp.where(i < NK, a, jnp.where(i < 2 * NK, b, 0.0)))
+    mix = jnp.concatenate(parts, axis=1)
+    high = mix.astype(BF16)
+    return jnp.concatenate([high, (mix - high.astype(F32)).astype(BF16)], axis=0)
+
+
+def exchange_body(here, green_ref, mix, own, below, above, mixed, packed, send_a, recv_a, send_b, recv_b, send_c, recv_c):
+    scatter(here, green_ref, own, send_a, lambda n: recv_a.at[n])
 
     def forward(n, _):
-        wait_tiles(here, 8, recv_a.at[n])
-        zs = lax.rem(z - ring_step(n) + NZ, NZ)
+        wait_tiles(own, 8, recv_a.at[n])
+        zs = around(here.z + NZ - ring_step(n), NZ)
         for core in range(2):
             rows = pl.ds(core * NK + zs * NX, NX)
-            for step, there, slot in ((1, below, 0), (NY - 1, above, 1)):
+            for there, land, slot in ((here.up, below, 0), (here.down, above, 1)):
                 pltpu.make_async_remote_copy(
-                    src_ref=here.at[rows],
-                    dst_ref=there.at[rows],
+                    src_ref=own.at[rows],
+                    dst_ref=land.at[rows],
                     send_sem=send_b.at[slot],
                     recv_sem=recv_b.at[slot],
-                    device_id=(lax.rem(y + step, NY) * 2 + c, z * NX + x),
+                    device_id=there,
                     device_id_type=MESH,
                 ).start()
         return 0
@@ -302,14 +325,12 @@
     wait_tiles(below, TILES, recv_b.at[0])
     wait_tiles(above, TILES, recv_b.at[1])
 
-    mix = mix_ref[...]
-    mix_high = mix.astype(BF16)
-    mix = jnp.concatenate([mix_high, (mix - mix_high.astype(F32)).astype(BF16)], axis=0)
     first = lax.broadcasted_iota(jnp.int32, (NK, W2), 1) < NORB
-    low = jnp.where(y > 0, 1.0, 0.0).astype(F32)
-    high = jnp.where(y < NY - 1, 1.0, 0.0).astype(F32)
-    flat = [r.reshape(TILES * 8, W2) for r in (below, here, above)]
+    low = jnp.where(here.y > 0, 1.0, 0.0).astype(F32)
+    high = jnp.where(here.y < NY - 1, 1.0, 0.0).astype(F32)
+    flat = [r.reshape(TILES * 8, W2) for r in (below, own, above)]
     out = mixed.reshape(TILES * 8, W2)
+    gap = jnp.zeros((W2 - 2 * NK, W2), F32)
     for s in range(8):
         t = []
         for r, keep in zip(flat, (low, None, high)):
@@ -323,66 +344,83 @@
             x2 = t[q + 1] + t[q - 1]
             x3 = jnp.where(first, w[q + 1] + w[q - 2], w[q + 2] + w[q - 1])
             x4 = t[q + 2] + t[q - 2]
-            xs = split(jnp.concatenate([x1, x2, x3, x4], axis=0))
+            xs = split(jnp.concatenate([x1, x2, gap, x3, x4, gap], axis=0))
             o = jnp.dot(mix, xs, preferred_element_type=F32)
             o = o[:, :W2] + o[:, W2:]
             out[pl.ds(core * NK * 8 + s, NK, stride=8), :] = o[:NK] + o[NK:]
 
-    scatter(mixed, sigma_ref, send_c, recv_c, False)
-    wait_tiles(here, TILES - 1, send_a)
+    scatter(here, mixed, packed, send_c, lambda n: recv_c)
+    wait_tiles(own, TILES - 1, send_a)
     wait_tiles(below, TILES, send_b.at[0])
     wait_tiles(above, TILES, send_b.at[1])
-    wait_tiles(sigma_ref, TILES, recv_c)
+    wait_tiles(packed, TILES, recv_c)
     wait_tiles(mixed, TILES - 1, send_c)
 
 
-def mix_rows(kernel, offsets):
-    steps = jnp.arange(1, NMODE + 1, dtype=jnp.int32)
-    chosen = jnp.where(offsets[None, :] == steps[:, None], 1.0, 0.0).astype(F32)
-    by_step = jnp.sum(chosen[:, :, None] * kernel[None, :, :], axis=1)
-    k = jnp.arange(NK, dtype=jnp.int32)
-    selector = (((k[:, None] - k[None, :]) % NK)[None] == k[:, None, None]).astype(F32)
-    return jnp.einsum("oq,qkj->koj", by_step, selector, precision=HIGHEST).reshape(NK, NMODE * NK)
-
-
-SCRATCH = [
-    pltpu.VMEM((TILES, 8, W2), F32),
-    pltpu.VMEM((TILES, 8, W2), F32),
-    pltpu.VMEM((TILES, 8, W2), F32),
-    pltpu.VMEM((TILES, 8, W2), F32),
-    pltpu.SemaphoreType.DMA,
-    pltpu.SemaphoreType.DMA((NZ,)),
-    pltpu.SemaphoreType.DMA((2,)),
-    pltpu.SemaphoreType.DMA((2,)),
-    pltpu.SemaphoreType.DMA,
-    pltpu.SemaphoreType.DMA,
-]
-
-
-def exchange_kernel(*refs):
-    greet()
+def step_kernel(counts_ref, offsets_ref, kernel_ref, onsite_hbm, hamil_hbm, coupling_hbm, lon_hbm, lhop_hbm,
+                sigma_ref, lead_ref,
+                onsite, hamil, coupling, lon, lhop, green, own, below, above, mixed, packed, l0_s, tf_s, ts_s, z0_s, sig_s,
+                load, send_a, recv_a, send_b, recv_b, send_c, recv_c):
+    moves = [
+        pltpu.make_async_copy(a, b, load.at[i])
+        for i, (a, b) in enumerate(
+            ((onsite_hbm, onsite), (lhop_hbm, lhop), (lon_hbm, lon), (coupling_hbm, coupling), (hamil_hbm, hamil))
+        )
+    ]
+    for move in moves:
+        move.start()
+    here = Place()
+    greet(here)
+    mix = mix_rows(kernel_ref, offsets_ref)
+
+    def loaded(stage):
+        for move in (moves[:1], moves[1:3], moves[3:])[stage]:
+            move.wait()
+
+    compute_body(counts_ref, onsite, hamil, coupling, lon, lhop, green, lead_ref, l0_s, tf_s, ts_s, z0_s, sig_s, loaded)
     all_greeted()
-    exchange_body(*refs)
-
-
-def exchange(green, mix):
+    exchange_body(here, green, mix, own, below, above, mixed, packed, send_a, recv_a, send_b, recv_b, send_c, recv_c)
+    for b in range(NB):
+        for part in range(2):
+            v = packed[pl.ds(b * 16 + part * 8, 8)].reshape(NORB, W2)
+            sigma_ref[0, b, part] = v[:, :NORB]
+            sigma_ref[1, b, part] = pltpu.roll(v, NORB, 1)[:, :NORB]
+
+
+def shards(onsite, hamil, coupling, lead_onsite, lead_hop, counts, kernel, offsets):
     vmem = pl.BlockSpec(memory_space=pltpu.VMEM)
-    return pl.pallas_call(
-        exchange_kernel,
-        name="exchange",
-        out_shape=jax.ShapeDtypeStruct((TILES, 8, W2), F32),
-        in_specs=[vmem] * 2,
-        out_specs=vmem,
-        scratch_shapes=SCRATCH,
-        compiler_params=pltpu.CompilerParams(collective_id=0, has_side_effects=True),
-    )(green, mix)
-
-
-def shards(onsite, hamil, coupling, lead_onsite, lead_hop, counts, kernel, offsets):
-    mix = mix_rows(kernel, offsets)
-    green, lead_sigma = compute(onsite, hamil, coupling, lead_onsite, lead_hop, counts)
-    sigma = exchange(green.reshape(TILES, 8, W2), mix)
-    sigma = sigma.reshape(NB, 2, NORB, 2, NORB).transpose(3, 0, 1, 2, 4)
+    smem = pl.BlockSpec(memory_space=pltpu.SMEM)
+    tiles = pltpu.VMEM((TILES, 8, W2), F32)
+    square = pltpu.VMEM((4, W2, W2), F32)
+    sigma, lead_sigma = pl.pallas_call(
+        step_kernel,
+        name="born_step",
+        out_shape=(
+            jax.ShapeDtypeStruct((2, NB, 2, NORB, NORB), F32),
+            jax.ShapeDtypeStruct((2, 2, 2, NORB, NORB), F32),
+        ),
+        in_specs=[smem, smem, vmem] + [pl.BlockSpec(memory_space=pl.ANY)] * 5,
+        out_specs=(vmem, vmem),
+        scratch_shapes=[
+            pltpu.VMEM((NB + 2, NORB), F32),
+            pltpu.VMEM((NB, 2, NORB, NORB), F32),
+            pltpu.VMEM((NB - 1, 2, NORB, NORB), F32),
+            pltpu.VMEM((2, 2, 2, NORB, NORB), F32),
+            pltpu.VMEM((2, 2, 2, NORB, NORB), F32),
+            tiles, tiles, tiles, tiles, tiles, tiles,
+            square, square, pltpu.VMEM((4, W2, 2 * W2), BF16), square, square,
+            pltpu.SemaphoreType.DMA((5,)),
+            pltpu.SemaphoreType.DMA,
+            pltpu.SemaphoreType.DMA((NZ,)),
+            pltpu.SemaphoreType.DMA((2,)),
+            pltpu.SemaphoreType.DMA((2,)),
+            pltpu.SemaphoreType.DMA,
+            pltpu.SemaphoreType.DMA,
+        ],
+        compiler_params=pltpu.CompilerParams(
+            collective_id=0, has_side_effects=True, vmem_limit_bytes=56 * 1024 * 1024
+        ),
+    )(counts, offsets, kernel, onsite[0], hamil[0], coupling[0], lead_onsite[:, 0], lead_hop[:, 0])
     return (sigma[:, None], lead_sigma[:, None])
 
 

time: 86.1 us -> 71.8 us (0.83)
  local copies, waits for them, and re-layouts: 9.11 us -> 2.84 us
  Pallas kernels: 73.7 us -> 68.1 us
  other arithmetic: 1.52 us -> 0 us
    pallas_call x2 -> x1, Pallas kernels: 73.7 us -> 68.1 us  [shards(): pl.pallas_call(step_kernel, name='born_step', out_shape=(jax.ShapeDtypeSt...]
    reshape x3 -> x0, local copies, waits for them, and re-layouts: 3.15 us -> none  [the longest x2 2.44 us: shards(): sigma = sigma.reshape(NB, 2, NORB, 2, NORB).transpose(3, 0, 1, 2, 4)]
    unnamed x14 -> x4, local copies, waits for them, and re-layouts: 5.95 us -> 2.84 us
where the time goes in v3:
time: 71.8 us; the launch traced here: 71.6 us
  Pallas kernels  68.1 us (95%)
  local copies, waits for them, and re-layouts  2.84 us (4%)
    pallas_call x1, Pallas kernels, shards(): pl.pallas_call(step_kernel, name='born_step', out_shape=(jax.ShapeDtypeSt...  68.1 us
    unnamed x4, local copies, waits for them, and re-layouts  2.84 us

profile of v3, /device:TPU:1, one launch (start us, length us, event | category | flops | bytes accessed | tf_op | source)
XLA Modules:
  0.0 71.6 jit_solution(15896982596341600336)
XLA Ops:
  0.6 68.1 %born_step.1 = (f32[2,6,2,64,64]{4,3,2,1,0:T(8,128)}, f32[2,2,2,64,64]{4,3,2,1,0:T(8,128)}) custom-call(s32[32]{0:T(128)} %counts_ref.1, s32[4]{0:T(128)} %offsets_ref.1, f32[4,48]{1,0:T(4,128)} %kernel_ref.1, f32[8,64]{1,0:T(8,128)} %bitcast.17, f32[6,2,64,64]{3,2,1,0:T(8,128)} %bitcast.12, f32[5,2,64,64]{3,2,1,0:T(8,128)} %bitcast.13, ...), custom_call_target="tpu_custom_call" | custom-call | tf_op jit(solution)/shard_map/born_step/pallas_call | solution.py:395
  68.7 0.0 copy-start
  68.8 2.1 %copy.14 = f32[2,1,6,2,64,64]{5,4,3,2,1,0:T(8,128)} copy(f32[2,1,6,2,64,64]{5,4,3,2,1,0:T(8,128)} %bitcast.11) | data formatting | bytes 786432
  70.9 0.0 copy-done
  70.9 0.7 copy.15
Async XLA Ops:
  68.7 2.1 %copy-start = (f32[2,2,2,64,64]{4,3,2,1,0:T(8,128)S(1)}, f32[2,2,2,64,64]{4,3,2,1,0:T(8,128)}, u32[]{:S(2)}) copy-start(f32[2,2,2,64,64]{4,3,2,1,0:T(8,128)} %get-tuple-element.5) | copy-start | bytes 393220

commit v4 on v3

--- a/solution.py
+++ b/solution.py
@@ -246,11 +246,13 @@
     pl.semaphore_wait(pltpu.get_barrier_semaphore(), TILES + 1)
 
 
-def scatter(here, src, dst, send_sem, recv_of):
+def scatter(here, half, src, dst, send_sem, recv_of):
+    rows = pl.ds(half * 4, 4)
+
     def send(n, zz, r):
         pltpu.make_async_remote_copy(
-            src_ref=src.at[here.tile(zz, r)],
-            dst_ref=dst.at[here.me],
+            src_ref=src.at[here.tile(zz, r), rows],
+            dst_ref=dst.at[here.me, rows],
             send_sem=send_sem,
             recv_sem=recv_of(n),
             device_id=here.device(zz, r),
@@ -266,11 +268,11 @@
     lax.fori_loop(0, NZ - 1, layer, 0)
     for r in range(1, 8):
         send(NZ - 1, here.z, r)
-    pltpu.make_async_copy(src.at[here.me], dst.at[here.me], recv_of(NZ - 1)).start()
-
-
-def wait_tiles(ref, count, sem):
-    part = ref.at[pl.ds(0, count)]
+    pltpu.make_async_copy(src.at[here.me, rows], dst.at[here.me, rows], recv_of(NZ - 1)).start()
+
+
+def wait_halves(ref, count, sem):
+    part = ref.at[pl.ds(0, count), pl.ds(0, 4)]
     pltpu.make_async_copy(part, part, sem).wait()
 
 
@@ -303,27 +305,8 @@
 
 
 def exchange_body(here, green_ref, mix, own, below, above, mixed, packed, send_a, recv_a, send_b, recv_b, send_c, recv_c):
-    scatter(here, green_ref, own, send_a, lambda n: recv_a.at[n])
-
-    def forward(n, _):
-        wait_tiles(own, 8, recv_a.at[n])
-        zs = around(here.z + NZ - ring_step(n), NZ)
-        for core in range(2):
-            rows = pl.ds(core * NK + zs * NX, NX)
-            for there, land, slot in ((here.up, below, 0), (here.down, above, 1)):
-                pltpu.make_async_remote_copy(
-                    src_ref=own.at[rows],
-                    dst_ref=land.at[rows],
-                    send_sem=send_b.at[slot],
-                    recv_sem=recv_b.at[slot],
-                    device_id=there,
-                    device_id_type=MESH,
-                ).start()
-        return 0
-
-    lax.fori_loop(0, NZ, forward, 0)
-    wait_tiles(below, TILES, recv_b.at[0])
-    wait_tiles(above, TILES, recv_b.at[1])
+    for half in range(2):
+        scatter(here, half, green_ref, own, send_a.at[half], lambda n: recv_a.at[half, n])
 
     first = lax.broadcasted_iota(jnp.int32, (NK, W2), 1) < NORB
     low = jnp.where(here.y > 0, 1.0, 0.0).astype(F32)
@@ -331,30 +314,53 @@
     flat = [r.reshape(TILES * 8, W2) for r in (below, own, above)]
     out = mixed.reshape(TILES * 8, W2)
     gap = jnp.zeros((W2 - 2 * NK, W2), F32)
-    for s in range(8):
-        t = []
-        for r, keep in zip(flat, (low, None, high)):
+
+    for half in range(2):
+
+        def forward(n, _):
+            wait_halves(own, 8, recv_a.at[half, n])
+            zs = around(here.z + NZ - ring_step(n), NZ)
             for core in range(2):
-                v = r[pl.ds(core * NK * 8 + s, NK, stride=8), :]
-                t.append(v if keep is None else v * keep)
-        w = [pltpu.roll(v, NORB, 1) for v in t]
-        for core in range(2):
-            q = 2 + core
-            x1 = w[q] + jnp.where(first, w[q - 1], w[q + 1])
-            x2 = t[q + 1] + t[q - 1]
-            x3 = jnp.where(first, w[q + 1] + w[q - 2], w[q + 2] + w[q - 1])
-            x4 = t[q + 2] + t[q - 2]
-            xs = split(jnp.concatenate([x1, x2, gap, x3, x4, gap], axis=0))
-            o = jnp.dot(mix, xs, preferred_element_type=F32)
-            o = o[:, :W2] + o[:, W2:]
-            out[pl.ds(core * NK * 8 + s, NK, stride=8), :] = o[:NK] + o[NK:]
-
-    scatter(here, mixed, packed, send_c, lambda n: recv_c)
-    wait_tiles(own, TILES - 1, send_a)
-    wait_tiles(below, TILES, send_b.at[0])
-    wait_tiles(above, TILES, send_b.at[1])
-    wait_tiles(packed, TILES, recv_c)
-    wait_tiles(mixed, TILES - 1, send_c)
+                part = (pl.ds(core * NK + zs * NX, NX), pl.ds(half * 4, 4))
+                for there, land, slot in ((here.up, below, 0), (here.down, above, 1)):
+                    pltpu.make_async_remote_copy(
+                        src_ref=own.at[part],
+                        dst_ref=land.at[part],
+                        send_sem=send_b.at[half, slot],
+                        recv_sem=recv_b.at[half, slot],
+                        device_id=there,
+                        device_id_type=MESH,
+                    ).start()
+            return 0
+
+        lax.fori_loop(0, NZ, forward, 0)
+        wait_halves(below, TILES, recv_b.at[half, 0])
+        wait_halves(above, TILES, recv_b.at[half, 1])
+        for s in range(half * 4, half * 4 + 4):
+            t = []
+            for r, keep in zip(flat, (low, None, high)):
+                for core in range(2):
+                    v = r[pl.ds(core * NK * 8 + s, NK, stride=8), :]
+                    t.append(v if keep is None else v * keep)
+            w = [pltpu.roll(v, NORB, 1) for v in t]
+            for core in range(2):
+                q = 2 + core
+                x1 = w[q] + jnp.where(first, w[q - 1], w[q + 1])
+                x2 = t[q + 1] + t[q - 1]
+                x3 = jnp.where(first, w[q + 1] + w[q - 2], w[q + 2] + w[q - 1])
+                x4 = t[q + 2] + t[q - 2]
+                xs = split(jnp.concatenate([x1, x2, gap, x3, x4, gap], axis=0))
+                o = jnp.dot(mix, xs, preferred_element_type=F32)
+                o = o[:, :W2] + o[:, W2:]
+                out[pl.ds(core * NK * 8 + s, NK, stride=8), :] = o[:NK] + o[NK:]
+        scatter(here, half, mixed, packed, send_c.at[half], lambda n: recv_c.at[half])
+
+    for half in range(2):
+        wait_halves(own, TILES - 1, send_a.at[half])
+        wait_halves(below, TILES, send_b.at[half, 0])
+        wait_halves(above, TILES, send_b.at[half, 1])
+        wait_halves(packed, TILES, recv_c.at[half])
+        wait_halves(mixed, TILES - 1, send_c.at[half])
 
 
 def step_kernel(counts_ref, offsets_ref, kernel_ref, onsite_hbm, hamil_hbm, coupling_hbm, lon_hbm, lhop_hbm,
@@ -410,12 +416,12 @@
             tiles, tiles, tiles, tiles, tiles, tiles,
             square, square, pltpu.VMEM((4, W2, 2 * W2), BF16), square, square,
             pltpu.SemaphoreType.DMA((5,)),
-            pltpu.SemaphoreType.DMA,
-            pltpu.SemaphoreType.DMA((NZ,)),
+            pltpu.SemaphoreType.DMA((2,)),
+            pltpu.SemaphoreType.DMA((2, NZ)),
+            pltpu.SemaphoreType.DMA((2, 2)),
+            pltpu.SemaphoreType.DMA((2, 2)),
             pltpu.SemaphoreType.DMA((2,)),
             pltpu.SemaphoreType.DMA((2,)),
-            pltpu.SemaphoreType.DMA,
-            pltpu.SemaphoreType.DMA,
         ],
         compiler_params=pltpu.CompilerParams(
             collective_id=0, has_side_effects=True, vmem_limit_bytes=56 * 1024 * 1024

time: 71.8 us -> 64.5 us (0.90)
  Pallas kernels: 68.1 us -> 60.8 us
    pallas_call x1, Pallas kernels: 68.1 us -> 60.8 us  [shards(): pl.pallas_call(step_kernel, name='born_step', out_shape=(jax.ShapeDtypeSt...]
where the time goes in v4:
time: 64.5 us; the launch traced here: 64.3 us
  Pallas kernels  60.8 us (94%)
  local copies, waits for them, and re-layouts  2.84 us (4%)
  between operations  0.65 us (1%)
    pallas_call x1, Pallas kernels, shards(): pl.pallas_call(step_kernel, name='born_step', out_shape=(jax.ShapeDtypeSt...  60.8 us
    unnamed x4, local copies, waits for them, and re-layouts  2.84 us

profile of v4, /device:TPU:1, one launch (start us, length us, event | category | flops | bytes accessed | tf_op | source)
XLA Modules:
  0.0 64.3 jit_solution(15512204644811969502)
XLA Ops:
  0.6 60.8 %born_step.1 = (f32[2,6,2,64,64]{4,3,2,1,0:T(8,128)}, f32[2,2,2,64,64]{4,3,2,1,0:T(8,128)}) custom-call(s32[32]{0:T(128)} %counts_ref.1, s32[4]{0:T(128)} %offsets_ref.1, f32[4,48]{1,0:T(4,128)} %kernel_ref.1, f32[8,64]{1,0:T(8,128)} %bitcast.17, f32[6,2,64,64]{3,2,1,0:T(8,128)} %bitcast.12, f32[5,2,64,64]{3,2,1,0:T(8,128)} %bitcast.13, ...), custom_call_target="tpu_custom_call" | custom-call | tf_op jit(solution)/shard_map/born_step/pallas_call | solution.py:401
  61.5 0.0 copy-start
  61.5 2.1 %copy.14 = f32[2,1,6,2,64,64]{5,4,3,2,1,0:T(8,128)} copy(f32[2,1,6,2,64,64]{5,4,3,2,1,0:T(8,128)} %bitcast.11) | data formatting | bytes 786432
  63.6 0.0 copy-done
  63.6 0.7 %copy.15 = f32[2,1,2,2,64,64]{5,4,3,2,1,0:T(8,128)} copy(f32[2,1,2,2,64,64]{5,4,3,2,1,0:T(8,128)S(1)} %bitcast.14) | data formatting | bytes 262144
Async XLA Ops:
  61.5 2.1 %copy-start = (f32[2,2,2,64,64]{4,3,2,1,0:T(8,128)S(1)}, f32[2,2,2,64,64]{4,3,2,1,0:T(8,128)}, u32[]{:S(2)}) copy-start(f32[2,2,2,64,64]{4,3,2,1,0:T(8,128)} %get-tuple-element.5) | copy-start | bytes 393220

commit v5 on v4

--- a/solution.py
+++ b/solution.py
@@ -304,10 +304,11 @@
     return jnp.concatenate([high, (mix - high.astype(F32)).astype(BF16)], axis=0)
 
 
-def exchange_body(here, green_ref, mix, own, below, above, mixed, packed, send_a, recv_a, send_b, recv_b, send_c, recv_c):
+def exchange_body(here, green_ref, mix_of, own, below, above, mixed, packed, send_a, recv_a, send_b, recv_b, send_c, recv_c):
     for half in range(2):
         scatter(here, half, green_ref, own, send_a.at[half], lambda n: recv_a.at[half, n])
 
+    mix = mix_of()
     first = lax.broadcasted_iota(jnp.int32, (NK, W2), 1) < NORB
     low = jnp.where(here.y > 0, 1.0, 0.0).astype(F32)
     high = jnp.where(here.y < NY - 1, 1.0, 0.0).astype(F32)
@@ -364,8 +365,8 @@
 
 
 def step_kernel(counts_ref, offsets_ref, kernel_ref, onsite_hbm, hamil_hbm, coupling_hbm, lon_hbm, lhop_hbm,
-                sigma_ref, lead_ref,
-                onsite, hamil, coupling, lon, lhop, green, own, below, above, mixed, packed, l0_s, tf_s, ts_s, z0_s, sig_s,
+                packed, lead_ref,
+                onsite, hamil, coupling, lon, lhop, green, own, below, above, mixed, l0_s, tf_s, ts_s, z0_s, sig_s,
                 load, send_a, recv_a, send_b, recv_b, send_c, recv_c):
     moves = [
         pltpu.make_async_copy(a, b, load.at[i])
@@ -377,7 +378,6 @@
         move.start()
     here = Place()
     greet(here)
-    mix = mix_rows(kernel_ref, offsets_ref)
 
     def loaded(stage):
         for move in (moves[:1], moves[1:3], moves[3:])[stage]:
@@ -385,12 +385,21 @@
 
     compute_body(counts_ref, onsite, hamil, coupling, lon, lhop, green, lead_ref, l0_s, tf_s, ts_s, z0_s, sig_s, loaded)
     all_greeted()
-    exchange_body(here, green, mix, own, below, above, mixed, packed, send_a, recv_a, send_b, recv_b, send_c, recv_c)
+    exchange_body(here, green, lambda: mix_rows(kernel_ref, offsets_ref), own, below, above, mixed, packed, send_a, recv_a, send_b, recv_b, send_c, recv_c)
+
+
+def unpack_kernel(packed, lead_in, sigma_hbm, lead_hbm, parts, sems):
+    moves = [pltpu.make_async_copy(lead_in, lead_hbm, sems.at[NB])]
+    moves[0].start()
     for b in range(NB):
         for part in range(2):
             v = packed[pl.ds(b * 16 + part * 8, 8)].reshape(NORB, W2)
-            sigma_ref[0, b, part] = v[:, :NORB]
-            sigma_ref[1, b, part] = pltpu.roll(v, NORB, 1)[:, :NORB]
+            parts[0, b, part] = v[:, :NORB]
+            parts[1, b, part] = pltpu.roll(v, NORB, 1)[:, :NORB]
+        moves.append(pltpu.make_async_copy(parts.at[:, b], sigma_hbm.at[:, b], sems.at[b]))
+        moves[-1].start()
+    for move in moves:
+        move.wait()
 
 
 def shards(onsite, hamil, coupling, lead_onsite, lead_hop, counts, kernel, offsets):
@@ -402,7 +411,7 @@
         step_kernel,
         name="born_step",
         out_shape=(
-            jax.ShapeDtypeStruct((2, NB, 2, NORB, NORB), F32),
+            jax.ShapeDtypeStruct((TILES, 8, W2), F32),
             jax.ShapeDtypeStruct((2, 2, 2, NORB, NORB), F32),
         ),
         in_specs=[smem, smem, vmem] + [pl.BlockSpec(memory_space=pl.ANY)] * 5,
@@ -413,7 +422,7 @@
             pltpu.VMEM((NB - 1, 2, NORB, NORB), F32),
             pltpu.VMEM((2, 2, 2, NORB, NORB), F32),
             pltpu.VMEM((2, 2, 2, NORB, NORB), F32),
-            tiles, tiles, tiles, tiles, tiles, tiles,
+            tiles, tiles, tiles, tiles, tiles,
             square, square, pltpu.VMEM((4, W2, 2 * W2), BF16), square, square,
             pltpu.SemaphoreType.DMA((5,)),
             pltpu.SemaphoreType.DMA((2,)),
@@ -427,6 +436,18 @@
             collective_id=0, has_side_effects=True, vmem_limit_bytes=56 * 1024 * 1024
         ),
     )(counts, offsets, kernel, onsite[0], hamil[0], coupling[0], lead_onsite[:, 0], lead_hop[:, 0])
+    anywhere = pl.BlockSpec(memory_space=pl.ANY)
+    sigma, lead_sigma = pl.pallas_call(
+        unpack_kernel,
+        name="unpack",
+        out_shape=(
+            jax.ShapeDtypeStruct((2, NB, 2, NORB, NORB), F32),
+            jax.ShapeDtypeStruct((2, 2, 2, NORB, NORB), F32),
+        ),
+        in_specs=[vmem, vmem],
+        out_specs=(anywhere, anywhere),
+        scratch_shapes=[pltpu.VMEM((2, NB, 2, NORB, NORB), F32), pltpu.SemaphoreType.DMA((NB + 1,))],
+    )(sigma, lead_sigma)
     return (sigma[:, None], lead_sigma[:, None])
 
 

time: 64.5 us -> 63.3 us (0.981)
  local copies, waits for them, and re-layouts: 2.84 us -> 0 us
  Pallas kernels: 60.8 us -> 62.5 us
    unnamed x4 -> x0, local copies, waits for them, and re-layouts: 2.84 us -> none
    pallas_call x0 -> x1, Pallas kernels: none -> 2.08 us  [shards(): pl.pallas_call(unpack_kernel, name='unpack', out_shape=(jax.ShapeDtypeStr...]
where the time goes in v5:
time: 63.3 us; the launch traced here: 63.1 us
  Pallas kernels  62.5 us (99%)
  between operations  0.64 us (1%)
    pallas_call x1, Pallas kernels, shards(): pl.pallas_call(step_kernel, name='born_step', out_shape=(jax.ShapeDtypeSt...  60.4 us
    pallas_call x1, Pallas kernels, shards(): pl.pallas_call(unpack_kernel, name='unpack', out_shape=(jax.ShapeDtypeStr...  2.08 us

profile of v5, /device:TPU:1, one launch (start us, length us, event | category | flops | bytes accessed | tf_op | source)
XLA Modules:
  0.0 63.1 jit_solution(15832136519674689702)
XLA Ops:
  0.6 60.4 %born_step.1 = (f32[96,8,128]{2,1,0:T(8,128)}, f32[2,2,2,64,64]{4,3,2,1,0:T(8,128)}) custom-call(s32[32]{0:T(128)} %counts_ref.1, s32[4]{0:T(128)} %offsets_ref.1, f32[4,48]{1,0:T(4,128)} %kernel_ref.1, f32[8,64]{1,0:T(8,128)} %bitcast.15, f32[6,2,64,64]{3,2,1,0:T(8,128)} %bitcast.11, f32[5,2,64,64]{3,2,1,0:T(8,128)} %bitcast.12, ...), custom_call_target="tpu_custom_call" | custom-call | tf_op jit(solution)/shard_map/born_step/pallas_call | solution.py:410
  61.0 2.1 %unpack.1 = (f32[2,6,2,64,64]{4,3,2,1,0:T(8,128)}, f32[2,2,2,64,64]{4,3,2,1,0:T(8,128)}) custom-call(f32[96,8,128]{2,1,0:T(8,128)} %get-tuple-element.6.packed, f32[2,2,2,64,64]{4,3,2,1,0:T(8,128)} %get-tuple-element.7.lead_in), custom_call_target="tpu_custom_call" | custom-call | tf_op jit(solution)/shard_map/unpack/pallas_call | solution.py:440
